TPU v7x, 512 devices: a whole 4x4x16 slice. The times are simulated.
512 devices in a mesh: sample: 4 (over z_hi), gx: 8 (over z_lo, core), gy: 4 (over x), gz: 4 (over y).
Axes of the slice: x: 4, y: 4, z: 16 (z_hi: 4, z_lo: 4; z = z_hi * 4 + z_lo), core: 2. Of those that a mesh axis runs over, the one named last changes fastest.
Arguments:
- volume: bfloat16 [64, 64, 64, 128], P(('sample', 'gx'), 'gy', 'gz'), parts along dimension 0, may hold values from -6 to 6
- conv4_weight: bfloat16 [3, 3, 3, 128, 256], replicated, may hold values from -0.109375 to 0.109375
- conv5_weight: bfloat16 [3, 3, 3, 256, 512], P(None, None, None, None, ('gy', 'gz')), may hold values from -0.078125 to 0.078125
Outputs:
- features: bfloat16 [32, 32, 32, 512], P(('sample', 'gx'), None, None, ('gy', 'gz')), parts along dimension 0
There are 4 independent parts, one for each index of `sample`. A program takes and returns all parts, laid end to end along the dimension named above; an argument that names none is the same for every part. Nothing has to cross between parts.
All inputs are finite; a program needn't handle non-finite values.
Results may differ from a plain program's by a relative error of at most 0.009.
Values may be sent and summed in bfloat16 or wider, within the bound.
A program may use at most 64 MiB of HBM per device.

v0:
```python
import jax
import jax.numpy as jnp
from jax import lax
from jax.sharding import PartitionSpec as P


def extended(cells, sides, width):
    for axis, dim in sides:
        count = lax.axis_size(axis)
        ends = count - 1
        head = lax.slice_in_dim(cells, 0, width, axis=dim)
        tail = lax.slice_in_dim(cells, cells.shape[dim] - width, cells.shape[dim], axis=dim)
        cells = jnp.concatenate(
            [
                lax.ppermute(tail, axis, [(i, (i + 1) % count) for i in range(ends)]),
                cells,
                lax.ppermute(head, axis, [((i + 1) % count, i) for i in range(ends)]),
            ],
            axis=dim,
        )
    return cells


def joined_along(tiles, dim):
    tiles = jnp.moveaxis(tiles, 0, dim)
    lengths = tiles.shape
    return tiles.reshape(*lengths[:dim], lengths[dim] * lengths[dim + 1], *lengths[dim + 2 :])


def sent_to_all(x, axis):
    copies = jnp.broadcast_to(x, (lax.axis_size(axis), *x.shape))
    return lax.all_to_all(copies, axis, split_axis=0, concat_axis=0, tiled=True)


def gather_directly(x, axis, dim):
    return joined_along(sent_to_all(x, axis), dim)


def conv_local(padded, kernel):
    extent_x = padded.shape[0] - 2
    extent_y = padded.shape[1] - 2
    extent_z = padded.shape[2] - 2
    inputs = padded.shape[3]
    summed = None
    for along_x in range(3):
        for along_y in range(3):
            for along_z in range(3):
                window = padded[
                    along_x : along_x + extent_x,
                    along_y : along_y + extent_y,
                    along_z : along_z + extent_z,
                ]
                window = window.reshape(extent_x * extent_y * extent_z, inputs)
                contrib = jnp.dot(
                    window, kernel[along_x, along_y, along_z], preferred_element_type=jnp.float32
                )
                summed = contrib if summed is None else summed + contrib
    return summed.reshape(extent_x, extent_y, extent_z, kernel.shape[4])


def pool_leaky(hidden):
    leaked = jnp.where(hidden > 0, hidden, 0.3 * hidden)
    sizes = leaked.shape
    blocks = leaked.reshape(sizes[0] // 2, 2, sizes[1] // 2, 2, sizes[2] // 2, 2, sizes[3])
    return jnp.max(blocks, axis=(1, 3, 5)).astype(jnp.bfloat16)


def body(volume, conv4_weight, conv5_weight):
    padded = extended(volume, (("gx", 0), ("gy", 1), ("gz", 2)), 1)
    pooled = pool_leaky(conv_local(padded, conv4_weight))
    strips = gather_directly(pooled, "gz", 2)
    slab = gather_directly(strips, "gy", 1)
    bordered = extended(slab, (("gx", 0),), 1)
    bordered = jnp.pad(bordered, ((0, 0), (1, 1), (1, 1), (0, 0)))
    return conv_local(bordered, conv5_weight).astype(jnp.bfloat16)


def solution(mesh):
    return jax.shard_map(
        body,
        mesh=mesh,
        in_specs=(
            P(("sample", "gx"), "gy", "gz", None),
            P(),
            P(None, None, None, None, ("gy", "gz")),
        ),
        out_specs=P(("sample", "gx"), None, None, ("gy", "gz")),
        check_vma=False,
    )
```

profile of v0, /device:TPU:1, one launch (start us, length us, event | category | flops | bytes accessed | tf_op | source)
XLA Modules:
  0.0 82.7 jit_solution(15706448101873972406)
XLA Ops:
  0.0 1.0 %fusion.183 = (bf16[1,16,16,128]{3,2,1,0:T(8,128)(2,1)S(1)}, bf16[1,16,16,128]{3,2,1,0:T(8,128)(2,1)S(1)}) fusion(bf16[2,16,16,128]{3,2,1,0:T(8,128)(2,1)} %param.3), kind=kLoop, calls=%fused_computation.235 | loop fusion | bytes 262144 | tf_op jit(solution)/shard_map/slice | solution.py:11
  1.0 4.9 %collective-permute-start = (bf16[1,16,16,128]{3,2,1,0:T(8,128)(2,1)S(1)}, bf16[1,16,16,128]{3,2,1,0:T(8,128)(2,1)S(1)}, u32[]{:S(2)}, u32[]{:S(2)}) collective-permute-start(bf16[1,16,16,128]{3,2,1,0:T(8,128)(2,1)S(1)} %get-tuple-element.66), channel_id=1, source_target_pairs={{0,16},{16,32},{32,48},{48,64},{64,80},{80,96},{96,112},{1,17},{17... | collective-permute-start | bytes 196616 | tf_op jit(solution)/shard_map/ppermute | solution.py:15
  5.9 5.1 %collective-permute-start.1 = (bf16[1,16,16,128]{3,2,1,0:T(8,128)(2,1)S(1)}, bf16[1,16,16,128]{3,2,1,0:T(8,128)(2,1)S(1)}, u32[]{:S(2)}, u32[]{:S(2)}) collective-permute-start(bf16[1,16,16,128]{3,2,1,0:T(8,128)(2,1)S(1)} %get-tuple-element.65), channel_id=1, source_target_pairs={{16,0},{32,16},{48,32},{64,48},{80,64},{96,80},{112,96},{17,1},{33... | collective-permute-start | bytes 196616 | tf_op jit(solution)/shard_map/ppermute | solution.py:17
  11.1 0.9 %collective-permute-done.1 = bf16[1,16,16,128]{3,2,1,0:T(8,128)(2,1)S(1)} collective-permute-done((bf16[1,16,16,128]{3,2,1,0:T(8,128)(2,1)S(1)}, bf16[1,16,16,128]{3,2,1,0:T(8,128)(2,1)S(1)}, u32[]{:S(2)}, u32[]{:S(2)}) %collective-permute-start.1) | collective-permute-done | bytes 65568 | tf_op jit(solution)/shard_map/ppermute | solution.py:17
  12.0 1.0 %pad_maximum_fusion.2 = (bf16[2,16,16,128]{3,2,1,0:T(8,128)(2,1)S(1)}, bf16[4,16,16,128]{3,2,1,0:T(8,128)(2,1)S(1)}, bf16[2,16,16,128]{3,2,1,0:T(8,128)(2,1)S(1)}) fusion(bf16[1,16,16,128]{3,2,1,0:T(8,128)(2,1)S(1)} %collective-permute-done.1, bf16[2,16,16,128]{3,2,1,0:T(8,128)(2,1)} %param.3, ...), kind=kLoop, calls=%fused_computation.82 | loop fusion | flops 524288 | bytes 655360 | tf_op jit(solution)/shard_map/concatenate | solution.py:13
  13.0 2.7 %collective-permute-start.2 = (bf16[4,1,16,128]{3,2,1,0:T(8,128)(2,1)S(1)}, bf16[4,1,16,128]{3,2,1,0:T(8,128)(2,1)S(1)}, u32[]{:S(2)}, u32[]{:S(2)}) collective-permute-start(bf16[4,1,16,128]{3,2,1,0:T(8,128)(2,1)S(1)} %get-tuple-element.60), channel_id=1, source_target_pairs={{0,4},{4,8},{8,12},{1,5},{5,9},{9,13},{2,6},{6,10},{10,14},{3,7},{... | collective-permute-start | bytes 49160 | tf_op jit(solution)/shard_map/ppermute | solution.py:15
  15.7 1.3 %collective-permute-start.3 = (bf16[4,1,16,128]{3,2,1,0:T(8,128)(2,1)S(1)}, bf16[4,1,16,128]{3,2,1,0:T(8,128)(2,1)S(1)}, u32[]{:S(2)}, u32[]{:S(2)}) collective-permute-start(bf16[4,1,16,128]{3,2,1,0:T(8,128)(2,1)S(1)} %get-tuple-element.61), channel_id=1, source_target_pairs={{4,0},{8,4},{12,8},{5,1},{9,5},{13,9},{6,2},{10,6},{14,10},{7,3},{... | collective-permute-start | bytes 49160 | tf_op jit(solution)/shard_map/ppermute | solution.py:17
  17.0 3.2 %collective-permute-done.3 = bf16[4,1,16,128]{3,2,1,0:T(8,128)(2,1)S(1)} collective-permute-done((bf16[4,1,16,128]{3,2,1,0:T(8,128)(2,1)S(1)}, bf16[4,1,16,128]{3,2,1,0:T(8,128)(2,1)S(1)}, u32[]{:S(2)}, u32[]{:S(2)}) %collective-permute-start.3) | collective-permute-done | bytes 16416 | tf_op jit(solution)/shard_map/ppermute | solution.py:17
  20.3 3.2 %collective-permute-start.4 = (bf16[4,18,1,128]{3,2,1,0:T(2,128)(2,1)S(1)}, bf16[4,18,1,128]{3,2,1,0:T(2,128)(2,1)S(1)}, u32[]{:S(2)}, u32[]{:S(2)}) collective-permute-start(bf16[4,18,1,128]{3,2,1,0:T(2,128)(2,1)S(1)} %get-tuple-element.49), channel_id=1, source_target_pairs={{0,1},{1,2},{2,3},{4,5},{5,6},{6,7},{8,9},{9,10},{10,11},{12,13},{... | collective-permute-start | bytes 55304 | tf_op jit(solution)/shard_map/ppermute | solution.py:15
  23.5 1.3 %collective-permute-start.5 = (bf16[4,18,1,128]{3,2,1,0:T(2,128)(2,1)S(1)}, bf16[4,18,1,128]{3,2,1,0:T(2,128)(2,1)S(1)}, u32[]{:S(2)}, u32[]{:S(2)}) collective-permute-start(bf16[4,18,1,128]{3,2,1,0:T(2,128)(2,1)S(1)} %get-tuple-element.50), channel_id=1, source_target_pairs={{1,0},{2,1},{3,2},{5,4},{6,5},{7,6},{9,8},{10,9},{11,10},{13,12},{... | collective-permute-start | bytes 55304 | tf_op jit(solution)/shard_map/ppermute | solution.py:17
  25.1 3.3 %collective-permute-done.5 = bf16[4,18,1,128]{3,2,1,0:T(2,128)(2,1)S(1)} collective-permute-done((bf16[4,18,1,128]{3,2,1,0:T(2,128)(2,1)S(1)}, bf16[4,18,1,128]{3,2,1,0:T(2,128)(2,1)S(1)}, u32[]{:S(2)}, u32[]{:S(2)}) %collective-permute-start.5) | collective-permute-done | bytes 18464 | tf_op jit(solution)/shard_map/ppermute | solution.py:17
  28.4 0.3 maximum_maximum_fusion
  28.7 0.3 fusion.180
  34.9 0.3 reshape.247
  35.2 0.5 fusion.35
  35.7 8.5 %all_to_all.10 = bf16[4,1,8,8,256]{4,3,2,1,0:T(8,128)(2,1)S(1)} all-to-all(bf16[4,1,8,8,256]{4,3,2,1,0:T(8,128)(2,1)S(1)} %broadcast_in_dim.6), channel_id=1, replica_groups=mesh['sample'=4,'gx'=8,'gy'=4,'gz'=4] {'gz'}, dimensions={0} | all-to-all | bytes 262144 | tf_op jit(solution)/shard_map/all_to_all | solution.py:32
  44.3 10.7 %all_to_all.11 = bf16[4,1,8,32,256]{4,3,2,1,0:T(8,128)(2,1)S(1)} all-to-all(bf16[4,1,8,32,256]{4,3,2,1,0:T(8,128)(2,1)S(1)} %broadcast_in_dim.7), channel_id=1, replica_groups=mesh['sample'=4,'gx'=8,'gy'=4,'gz'=4] {'gy'}, dimensions={0} | all-to-all | bytes 1048576 | tf_op jit(solution)/shard_map/all_to_all | solution.py:32
  55.0 5.1 %collective-permute-start.7 = (bf16[1,32,32,256]{3,2,1,0:T(8,128)(2,1)S(1)}, bf16[1,32,32,256]{3,2,1,0:T(8,128)(2,1)S(1)}, u32[]{:S(2)}, u32[]{:S(2)}) collective-permute-start(bf16[1,32,32,256]{3,2,1,0:T(8,128)(2,1)S(1)} %bitcast.277), channel_id=1, source_target_pairs={{16,0},{32,16},{48,32},{64,48},{80,64},{96,80},{112,96},{17,1},{33... | collective-permute-start | bytes 1572872 | tf_op jit(solution)/shard_map/ppermute | solution.py:17
  60.1 3.9 %collective-permute-start.6 = (bf16[1,32,32,256]{3,2,1,0:T(8,128)(2,1)S(1)}, bf16[1,32,32,256]{3,2,1,0:T(8,128)(2,1)S(1)}, u32[]{:S(2)}, u32[]{:S(2)}) collective-permute-start(bf16[1,32,32,256]{3,2,1,0:T(8,128)(2,1)S(1)} %bitcast.278), channel_id=1, source_target_pairs={{0,16},{16,32},{32,48},{48,64},{64,80},{80,96},{96,112},{1,17},{17... | collective-permute-start | bytes 1572872 | tf_op jit(solution)/shard_map/ppermute | solution.py:15
  64.3 4.7 %collective-permute-done.7 = bf16[1,32,32,256]{3,2,1,0:T(8,128)(2,1)S(1)} collective-permute-done((bf16[1,32,32,256]{3,2,1,0:T(8,128)(2,1)S(1)}, bf16[1,32,32,256]{3,2,1,0:T(8,128)(2,1)S(1)}, u32[]{:S(2)}, u32[]{:S(2)}) %collective-permute-start.7) | collective-permute-done | bytes 524320 | tf_op jit(solution)/shard_map/ppermute | solution.py:17
  69.0 1.2 %collective-permute-done.6 = bf16[1,32,32,256]{3,2,1,0:T(8,128)(2,1)S(1)} collective-permute-done((bf16[1,32,32,256]{3,2,1,0:T(8,128)(2,1)S(1)}, bf16[1,32,32,256]{3,2,1,0:T(8,128)(2,1)S(1)}, u32[]{:S(2)}, u32[]{:S(2)}) %collective-permute-start.6) | collective-permute-done | bytes 524320 | tf_op jit(solution)/shard_map/ppermute | solution.py:15
  70.1 1.0 %select_maximum_fusion = bf16[3,34,34,256]{3,2,1,0:T(8,128)(2,1)S(1)} fusion(bf16[1,32,32,256]{3,2,1,0:T(8,128)(2,1)S(1)} %collective-permute-done.7, bf16[1,32,32,256]{3,2,1,0:T(8,128)(2,1)S(1)} %bitcast.280, bf16[1,32,32,256]{3,2,1,0:T(8,128)(2,1)S(1)} %collective-permute-done.6), kind=kLoop, calls=%fused_computation.8 | loop fusion | flops 16868352 | bytes 3348480 | tf_op jit(solution)/shard_map/concatenate | solution.py:13
  71.2 0.7 fusion.179
  71.8 3.0 %fusion.178 = (bf16[1,32,32,256]{3,2,1,0:T(8,128)(2,1)S(1)}, bf16[1,32,32,256]{3,2,1,0:T(8,128)(2,1)S(1)}, bf16[1,32,32,256]{3,2,1,0:T(8,128)(2,1)S(1)}, bf16[1,...) fusion(bf16[3,34,34,256]{3,2,1,0:T(8,128)(2,1)S(1)} %select_max, ...), kind=kLoop, calls=%fused_computation.230 | loop fusion | bytes 19922944 | tf_op jit(solution)/shard_map/slice | solution.py:48
  75.1 0.3 fusion.142
  75.6 0.3 fusion.146
  75.9 0.3 fusion.148
  76.7 0.3 fusion.103
  77.5 0.3 fusion.111
  81.2 0.3 fusion.32
  81.5 0.3 fusion.34
  81.8 0.8 %copy.8 = bf16[1024,32]{1,0:T(8,128)(2,1)} copy(bf16[1024,32]{0,1:T(8,128)(2,1)S(1)} %fusion.34) | data formatting | bytes 131072 | tf_op jit(solution)/shard_map/convert_element_type | solution.py:75
  (64 shorter events, 11.4 us)
Async XLA Ops:
  0.0 24.8 %copy-start = (bf16[3,3,3,128,256]{4,3,2,1,0:T(8,128)(2,1)S(1)}, bf16[3,3,3,128,256]{4,3,2,1,0:T(8,128)(2,1)}, u32[]{:S(2)}) copy-start(bf16[3,3,3,128,256]{4,3,2,1,0:T(8,128)(2,1)} %param.4) | copy-start | bytes 5308420
  1.0 10.1 %collective-permute-start = (bf16[1,16,16,128]{3,2,1,0:T(8,128)(2,1)S(1)}, bf16[1,16,16,128]{3,2,1,0:T(8,128)(2,1)S(1)}, u32[]{:S(2)}, u32[]{:S(2)}) collective-permute-start(bf16[1,16,16,128]{3,2,1,0:T(8,128)(2,1)S(1)} %get-tuple-element.66), channel_id=1, source_target_pairs={{0,16},{16,32},{32,48},{48,64},{64,80},{80,96},{96,112},{1,17},{17... | collective-permute-start | bytes 196616 | tf_op jit(solution)/shard_map/ppermute | solution.py:15
  5.9 6.0 %collective-permute-start.1 = (bf16[1,16,16,128]{3,2,1,0:T(8,128)(2,1)S(1)}, bf16[1,16,16,128]{3,2,1,0:T(8,128)(2,1)S(1)}, u32[]{:S(2)}, u32[]{:S(2)}) collective-permute-start(bf16[1,16,16,128]{3,2,1,0:T(8,128)(2,1)S(1)} %get-tuple-element.65), channel_id=1, source_target_pairs={{16,0},{32,16},{48,32},{64,48},{80,64},{96,80},{112,96},{17,1},{33... | collective-permute-start | bytes 196616 | tf_op jit(solution)/shard_map/ppermute | solution.py:17
  13.0 4.0 %collective-permute-start.2 = (bf16[4,1,16,128]{3,2,1,0:T(8,128)(2,1)S(1)}, bf16[4,1,16,128]{3,2,1,0:T(8,128)(2,1)S(1)}, u32[]{:S(2)}, u32[]{:S(2)}) collective-permute-start(bf16[4,1,16,128]{3,2,1,0:T(8,128)(2,1)S(1)} %get-tuple-element.60), channel_id=1, source_target_pairs={{0,4},{4,8},{8,12},{1,5},{5,9},{9,13},{2,6},{6,10},{10,14},{3,7},{... | collective-permute-start | bytes 49160 | tf_op jit(solution)/shard_map/ppermute | solution.py:15
  15.7 4.5 %collective-permute-start.3 = (bf16[4,1,16,128]{3,2,1,0:T(8,128)(2,1)S(1)}, bf16[4,1,16,128]{3,2,1,0:T(8,128)(2,1)S(1)}, u32[]{:S(2)}, u32[]{:S(2)}) collective-permute-start(bf16[4,1,16,128]{3,2,1,0:T(8,128)(2,1)S(1)} %get-tuple-element.61), channel_id=1, source_target_pairs={{4,0},{8,4},{12,8},{5,1},{9,5},{13,9},{6,2},{10,6},{14,10},{7,3},{... | collective-permute-start | bytes 49160 | tf_op jit(solution)/shard_map/ppermute | solution.py:17
  20.3 4.8 %collective-permute-start.4 = (bf16[4,18,1,128]{3,2,1,0:T(2,128)(2,1)S(1)}, bf16[4,18,1,128]{3,2,1,0:T(2,128)(2,1)S(1)}, u32[]{:S(2)}, u32[]{:S(2)}) collective-permute-start(bf16[4,18,1,128]{3,2,1,0:T(2,128)(2,1)S(1)} %get-tuple-element.49), channel_id=1, source_target_pairs={{0,1},{1,2},{2,3},{4,5},{5,6},{6,7},{8,9},{9,10},{10,11},{12,13},{... | collective-permute-start | bytes 55304 | tf_op jit(solution)/shard_map/ppermute | solution.py:15
  23.5 4.9 %collective-permute-start.5 = (bf16[4,18,1,128]{3,2,1,0:T(2,128)(2,1)S(1)}, bf16[4,18,1,128]{3,2,1,0:T(2,128)(2,1)S(1)}, u32[]{:S(2)}, u32[]{:S(2)}) collective-permute-start(bf16[4,18,1,128]{3,2,1,0:T(2,128)(2,1)S(1)} %get-tuple-element.50), channel_id=1, source_target_pairs={{1,0},{2,1},{3,2},{5,4},{6,5},{7,6},{9,8},{10,9},{11,10},{13,12},{... | collective-permute-start | bytes 55304 | tf_op jit(solution)/shard_map/ppermute | solution.py:17
  31.6 0.9 %copy-start.1 = (bf16[2,16,16,128]{3,2,1,0:T(8,128)(2,1)S(1)}, bf16[2,16,16,128]{3,2,1,0:T(8,128)(2,1)}, u32[]{:S(2)}) copy-start(bf16[2,16,16,128]{3,2,1,0:T(8,128)(2,1)} %param.3) | copy-start | bytes 393220
  34.9 29.2 %copy-start.2 = (bf16[3,3,3,256,32]{3,4,2,1,0:T(8,128)(2,1)S(1)}, bf16[3,3,3,256,32]{3,4,2,1,0:T(8,128)(2,1)}, u32[]{:S(2)}) copy-start(bf16[3,3,3,256,32]{3,4,2,1,0:T(8,128)(2,1)} %param.5) | copy-start | bytes 1327108
  55.0 14.0 %collective-permute-start.7 = (bf16[1,32,32,256]{3,2,1,0:T(8,128)(2,1)S(1)}, bf16[1,32,32,256]{3,2,1,0:T(8,128)(2,1)S(1)}, u32[]{:S(2)}, u32[]{:S(2)}) collective-permute-start(bf16[1,32,32,256]{3,2,1,0:T(8,128)(2,1)S(1)} %bitcast.277), channel_id=1, source_target_pairs={{16,0},{32,16},{48,32},{64,48},{80,64},{96,80},{112,96},{17,1},{33... | collective-permute-start | bytes 1572872 | tf_op jit(solution)/shard_map/ppermute | solution.py:17
  60.1 10.0 %collective-permute-start.6 = (bf16[1,32,32,256]{3,2,1,0:T(8,128)(2,1)S(1)}, bf16[1,32,32,256]{3,2,1,0:T(8,128)(2,1)S(1)}, u32[]{:S(2)}, u32[]{:S(2)}) collective-permute-start(bf16[1,32,32,256]{3,2,1,0:T(8,128)(2,1)S(1)} %bitcast.278), channel_id=1, source_target_pairs={{0,16},{16,32},{32,48},{48,64},{64,80},{80,96},{96,112},{1,17},{17... | collective-permute-start | bytes 1572872 | tf_op jit(solution)/shard_map/ppermute | solution.py:15
where the time goes:
time: 83.1 us; the launch traced here: 82.7 us
  starting transfers between devices  27.6 us (33%)
  blocking collectives  19.2 us (23%)
  waiting for transfers between devices  13.2 us (16%)
  matrix products  12.8 us (15%)
  local copies, waits for them, and re-layouts  6.46 us (8%)
  other arithmetic  2.93 us (4%)
    all_to_all x2, blocking collectives, sent_to_all(): return lax.all_to_all(copies, axis, split_axis=0, concat_axis=0, tiled=True)  19.2 us
    ppermute x4, starting transfers between devices, extended(): lax.ppermute(tail, axis, [(i, (i + 1) % count) for i in range(ends)])  14.7 us
    ppermute x4, starting transfers between devices, extended(): lax.ppermute(head, axis, [((i + 1) % count, i) for i in range(ends)])  12.8 us
    dot_general x54, matrix products, conv_local(): jnp.dot(window, kernel[along_x, along_y, along_z], preferred_element_type...  12.8 us
    ppermute x4, waiting for transfers between devices, extended(): lax.ppermute(head, axis, [((i + 1) % count, i) for i in range(ends)])  12 us
    slice x3, local copies, waits for them, and re-layouts, conv_local(): padded[along_x:along_x + extent_x, along_y:along_y + extent_y, along_z:al...  3.95 us
    concatenate x4, other arithmetic, extended(): jnp.concatenate([lax.ppermute(tail, axis, [(i, (i + 1) % count) for i in...  2.42 us
  transfers between devices with their start and end apart: 8, of which 5 were waited for; matrix products, arithmetic and copies ran while one was open for 1% of the time, Pallas kernels for 0%

commit v1 on v0

v1 whole, which is shorter than its diff:
```python
import functools

import jax
import jax.numpy as jnp
from jax import lax
from jax.experimental import pallas as pl
from jax.experimental.pallas import tpu as pltpu
from jax.sharding import PartitionSpec as P

MESH = pl.DeviceIdType.MESH
BF16, F32 = jnp.bfloat16, jnp.float32
CIN, C4, FILTERS = 128, 256, 32
PLANE = 32
SHIFTS = [(i, j, k) for i in (-1, 0, 1) for j in (-1, 0, 1) for k in (-1, 0, 1) if (i, j, k) != (0, 0, 0)]


def kernel(
    sizes, v, w4, w5, out,
    pad, wide, taps, w4b, w5b, zs, yz, zh, ch, pool, block, blocks, slab, edge, sent, got, packed,
    load_sem, halo_send, halo_recv, block_send, block_recv, part_send, part_recv,
):
    ngx, ngy, ngz = sizes
    g, a, b = lax.axis_index("gx"), lax.axis_index("gy"), lax.axis_index("gz")

    def there(dg, da, db):
        ok = None
        for at, step, n in ((g, dg, ngx), (a, da, ngy), (b, db, ngz)):
            if step:
                fine = (at > 0) if step < 0 else (at < n - 1)
                ok = fine if ok is None else jnp.logical_and(ok, fine)
        return ok

    def device(dg, da, db):
        return {"gx": g + dg, "gy": a + da, "gz": b + db}

    own_load = pltpu.make_async_copy(v, pad.at[1:3, 1:17], load_sem.at[0])
    own_load.start()
    w4_load = pltpu.make_async_copy(w4, w4b, load_sem.at[1])
    w4_load.start()
    w5_loads = []
    for dx in range(3):
        for dy in range(3):
            w5_loads.append(
                pltpu.make_async_copy(
                    w5.at[dx, dy],
                    w5b.at[:, dx * FILTERS : (dx + 1) * FILTERS, dy * C4 : (dy + 1) * C4],
                    load_sem.at[2 + dx * 3 + dy],
                )
            )
    for load in w5_loads:
        load.start()

    barrier = pltpu.get_barrier_semaphore()
    for da in range(ngy):
        for db in range(ngz):
            if (da, db) != (0, 0):
                pl.semaphore_signal(
                    barrier, inc=1, device_id={"gy": lax.rem(a + da, ngy), "gz": lax.rem(b + db, ngz)}, device_id_type=MESH
                )
    for shift in SHIFTS:
        if shift[0]:
            @pl.when(there(*shift))
            def _():
                pl.semaphore_signal(barrier, inc=1, device_id=device(*shift), device_id_type=MESH)

    def near(at, n):
        return jnp.int32(1) + (at > 0).astype(jnp.int32) + (at < n - 1).astype(jnp.int32)

    greeted = (near(g, ngx) - 1) * near(a, ngy) * near(b, ngz) + (ngy * ngz - 1)

    @pl.when(g == 0)
    def _():
        pad[0] = jnp.zeros(pad.shape[1:], BF16)
        zh[:, 0] = jnp.zeros((2, 16, CIN), BF16)
        ch[:, :, 0] = jnp.zeros((2, 2, 8, CIN), F32)

    @pl.when(g == ngx - 1)
    def _():
        pad[3] = jnp.zeros(pad.shape[1:], BF16)
        zh[:, 3] = jnp.zeros((2, 16, CIN), BF16)
        ch[:, :, 2] = jnp.zeros((2, 2, 8, CIN), F32)

    for side, edge_at in ((0, 0), (1, ngy - 1)):
        @pl.when(a == edge_at)
        def _():
            pad[:, 17 * side] = jnp.zeros((4, 16, CIN), BF16)
            ch[:, side] = jnp.zeros((2, 3, 8, CIN), F32)

    for side, edge_at in ((0, 0), (1, ngz - 1)):
        @pl.when(b == edge_at)
        def _():
            zh[side] = jnp.zeros((4, 16, CIN), BF16)
            ch[side] = jnp.zeros((2, 3, 8, CIN), F32)

    slab[0] = jnp.zeros((PLANE, C4), BF16)
    slab[PLANE + 1] = jnp.zeros((PLANE, C4), BF16)
    w5b[:, 96:128, :] = jnp.zeros((3, 32, 3 * C4), BF16)
    edge[:, :, 0:8] = jnp.zeros((2, 8, 8, 128), F32)
    edge[:, :, 40:48] = jnp.zeros((2, 8, 8, 128), F32)
    yz[...] = jnp.zeros(yz.shape, F32)

    own_load.wait()
    for x in (1, 2):
        for y in range(1, 17):
            row = (x * 18 + y) * 32 + 8
            wide[row : row + 16, :] = pad[x, y].astype(F32)
    for side, z in ((0, 0), (1, 15)):
        for x in (0, 1):
            first = ((x + 1) * 18 + 1) * 32 + 8 + z
            column = wide[pl.ds(first, 16, stride=32), :]
            zs[side, x] = column.astype(BF16)
            for ys, y in ((0, 0), (1, 15)):
                yz[side, ys, x : x + 1, :] = column[y : y + 1]

    pl.semaphore_wait(barrier, greeted)

    def halo(shift):
        dg, da, db = shift
        x = {-1: 0, 1: 1}.get(dg)
        px = {-1: 3, 1: 0}.get(dg)
        y = {-1: 0, 1: 15}.get(da)
        py = {-1: 17, 1: 0}.get(da)
        s = {-1: 0, 1: 1}.get(db)
        if db == 0:
            if da == 0:
                src, dst = pad.at[x + 1, 1:17], pad.at[px, 1:17]
            elif dg == 0:
                src, dst = pad.at[1:3, y + 1], pad.at[1:3, py]
            else:
                src, dst = pad.at[x + 1, y + 1], pad.at[px, py]
        elif da == 0:
            if dg == 0:
                src, dst = zs.at[s], zh.at[1 - s, 1:3]
            else:
                src, dst = zs.at[s, x], zh.at[1 - s, px]
        else:
            ys = {-1: 0, 1: 1}[da]
            src, dst = yz.at[s, ys], ch.at[1 - s, 1 - ys, {-1: 2, 0: 1, 1: 0}[dg]]
        number = SHIFTS.index(shift)
        return pltpu.make_async_remote_copy(
            src_ref=src, dst_ref=dst, send_sem=halo_send.at[number], recv_sem=halo_recv.at[number],
            device_id=device(*shift), device_id_type=MESH,
        )

    for shift in SHIFTS:
        @pl.when(there(*shift))
        def _():
            halo(shift).start()
    for shift in SHIFTS:
        @pl.when(there(*(-i for i in shift)))
        def _():
            halo(shift).wait_recv()

    for x in range(4):
        for y in range(18):
            if not (x in (1, 2) and 1 <= y <= 16):
                row = (x * 18 + y) * 32 + 8
                wide[row : row + 16, :] = pad[x, y].astype(F32)
        for side, at in ((0, 7), (1, 24)):
            wide[pl.ds((x * 18 + 1) * 32 + at, 16, stride=32), :] = zh[side, x].astype(F32)
            for ys, y in ((0, 0), (1, 17)):
                source, row = ((0, 1), (1, 0), (1, 1), (2, 0))[x]
                first = (x * 18 + y) * 32 + at
                wide[first : first + 1, :] = ch[side, ys, source, row : row + 1, :]
    for x in range(4):
        for y in range(18):
            row = (x * 18 + y) * 32
            left = wide[row + 7 : row + 23, :].astype(BF16)
            right = wide[row + 9 : row + 25, :].astype(BF16)
            taps[x, y * 16 : y * 16 + 16, :] = jnp.concatenate([left, pad[x, y], right], axis=-1)

    w4_load.wait()
    for part in range(4):
        tops = None
        for x in (0, 1):
            lhs = jnp.concatenate(
                [taps[x + dx, (4 * part + dy) * 16 : (4 * part + dy) * 16 + 64, :] for dx in range(3) for dy in range(3)], axis=-1
            )
            hidden = jnp.dot(lhs, w4b[...], preferred_element_type=F32)
            tops = hidden if tops is None else jnp.maximum(tops, hidden)
        tops = jnp.max(tops.reshape(2, 2, 16, C4), axis=1).reshape(32, C4)
        for half in range(2):
            pool[half, part * 32 : part * 32 + 32, :] = tops[:, half * 128 : half * 128 + 128]
    for half in range(2):
        tops = jnp.maximum(pool[half, pl.ds(0, 64, stride=2), :], pool[half, pl.ds(1, 64, stride=2), :])
        block[:, half * 128 : half * 128 + 128] = jnp.where(tops > 0, tops, 0.3 * tops).astype(BF16)

    me = a * ngz + b
    offsets = [(da, db) for da in range(ngy) for db in range(ngz) if (da, db) != (0, 0)]

    def spread(da, db):
        number = da * ngz + db
        return pltpu.make_async_remote_copy(
            src_ref=block, dst_ref=blocks.at[me], send_sem=block_send.at[number], recv_sem=block_recv.at[number],
            device_id={"gy": lax.rem(a + da, ngy), "gz": lax.rem(b + db, ngz)}, device_id_type=MESH,
        )

    for da, db in offsets:
        spread(da, db).start()
    blocks[me] = block[...]
    for load in w5_loads:
        load.wait()
    for da, db in offsets:
        spread(da, db).wait_recv()

    for row in range(ngy):
        for pair in range(2):
            halves = [blocks[row * ngz + 2 * pair + i].astype(F32).reshape(8, 1, 8, C4) for i in range(2)]
            tile = jnp.concatenate(halves, axis=1).reshape(8, 16, C4).astype(BF16)
            slab[1 + 8 * row : 9 + 8 * row, 16 * pair : 16 * pair + 16, :] = tile

    def part_copy(q, k):
        dg = 1 if k == 0 else -1
        return pltpu.make_async_remote_copy(
            src_ref=sent.at[k, q], dst_ref=got.at[k, q], send_sem=part_send.at[k, q], recv_sem=part_recv.at[k, q],
            device_id={"gx": g + dg}, device_id_type=MESH,
        )

    lane = lax.broadcasted_iota(jnp.int32, (64, 128), 1)

    def group(rows, k):
        moved = [
            rows[64 * u : 64 * u + 64] if u == k else pltpu.roll(rows[64 * u : 64 * u + 64], (32 * (u - k)) % 128, axis=1)
            for u in range(4)
        ]
        return jnp.where(lane < 64, jnp.where(lane < 32, moved[0], moved[1]), jnp.where(lane < 96, moved[2], moved[3]))

    for q in range(4):
        lhs = jnp.concatenate([slab[8 * q + dy : 8 * q + dy + 8].reshape(256, C4) for dy in range(3)], axis=-1)
        sums = [
            lax.dot_general(lhs, w5b[dz], (((1,), (1,)), ((), ())), preferred_element_type=F32).reshape(8, PLANE, 128)
            for dz in range(3)
        ]
        edge[0, :, 8:40] = sums[0]
        edge[1, :, 8:40] = sums[2]
        total = (sums[1] + edge[0, :, 7:39] + edge[1, :, 9:41]).reshape(256, 128)
        sent[0, q] = group(total, 0).astype(BF16)
        sent[1, q] = group(total, 2).astype(BF16)

        @pl.when(g < ngx - 1)
        def _():
            part_copy(q, 0).start()

        @pl.when(g > 0)
        def _():
            part_copy(q, 1).start()

        packed[q] = group(total, 1)

    @pl.when(g > 0)
    def _():
        for q in range(4):
            part_copy(q, 0).wait_recv()
            packed[q] += got[0, q].astype(F32)

    @pl.when(g < ngx - 1)
    def _():
        for q in range(4):
            part_copy(q, 1).wait_recv()
            packed[q] += got[1, q].astype(F32)

    out[...] = packed[...].astype(BF16)

    for shift in SHIFTS:
        @pl.when(there(*shift))
        def _():
            halo(shift).wait_send()
    for da, db in offsets:
        spread(da, db).wait_send()

    @pl.when(g < ngx - 1)
    def _():
        for q in range(4):
            part_copy(q, 0).wait_send()

    @pl.when(g > 0)
    def _():
        for q in range(4):
            part_copy(q, 1).wait_send()


def body(sizes, volume, conv4_weight, conv5_weight):
    ngx, ngy, ngz = sizes
    any_space = pl.BlockSpec(memory_space=pl.ANY)
    packed = pl.pallas_call(
        functools.partial(kernel, sizes),
        out_shape=jax.ShapeDtypeStruct((4, 64, 128), BF16),
        in_specs=[any_space] * 3,
        out_specs=pl.BlockSpec(memory_space=pltpu.VMEM),
        scratch_shapes=[
            pltpu.VMEM((4, 18, 16, CIN), BF16),
            pltpu.VMEM((4 * 18 * 32, CIN), F32),
            pltpu.VMEM((4, 18 * 16, 3 * CIN), BF16),
            pltpu.VMEM((27 * CIN, C4), BF16),
            pltpu.VMEM((3, 128, 3 * C4), BF16),
            pltpu.VMEM((2, 2, 16, CIN), BF16),
            pltpu.VMEM((2, 2, 8, CIN), F32),
            pltpu.VMEM((2, 4, 16, CIN), BF16),
            pltpu.VMEM((2, 2, 3, 8, CIN), F32),
            pltpu.VMEM((2, 128, 128), F32),
            pltpu.VMEM((64, C4), BF16),
            pltpu.VMEM((ngy * ngz, 64, C4), BF16),
            pltpu.VMEM((PLANE + 2, PLANE, C4), BF16),
            pltpu.VMEM((2, 8, 48, 128), F32),
            pltpu.VMEM((2, 4, 64, 128), BF16),
            pltpu.VMEM((2, 4, 64, 128), BF16),
            pltpu.VMEM((4, 64, 128), F32),
            pltpu.SemaphoreType.DMA((11,)),
            pltpu.SemaphoreType.DMA((26,)),
            pltpu.SemaphoreType.DMA((26,)),
            pltpu.SemaphoreType.DMA((ngy * ngz,)),
            pltpu.SemaphoreType.DMA((ngy * ngz,)),
            pltpu.SemaphoreType.DMA((2, 4)),
            pltpu.SemaphoreType.DMA((2, 4)),
        ],
        compiler_params=pltpu.CompilerParams(
            collective_id=0, has_side_effects=True, vmem_limit_bytes=40 * 1024 * 1024
        ),
    )(
        volume,
        conv4_weight.reshape(27 * CIN, C4),
        jnp.swapaxes(conv5_weight, 3, 4),
    )
    cells = packed.reshape(4, 2, PLANE, 4, FILTERS).transpose(0, 3, 1, 2, 4)
    return cells.reshape(1, PLANE, PLANE, FILTERS)


def solution(mesh):
    sizes = (mesh.shape["gx"], mesh.shape["gy"], mesh.shape["gz"])
    return jax.shard_map(
        functools.partial(body, sizes),
        mesh=mesh,
        in_specs=(
            P(("sample", "gx"), "gy", "gz", None),
            P(),
            P(None, None, None, None, ("gy", "gz")),
        ),
        out_specs=P(("sample", "gx"), None, None, ("gy", "gz")),
        check_vma=False,
    )
```

time: 83.1 us -> 37 us (0.45)
  Pallas kernels: 0 us -> 32.5 us
  starting transfers between devices: 27.6 us -> 0 us
  blocking collectives: 19.2 us -> 0 us
  waiting for transfers between devices: 13.2 us -> 0 us
  matrix products: 12.8 us -> 0 us
  other arithmetic: 2.93 us -> 0 us
  local copies, waits for them, and re-layouts: 6.46 us -> 4.3 us
    pallas_call x0 -> x1, Pallas kernels: none -> 32.5 us  [body(): pl.pallas_call(functools.partial(kernel, sizes), out_shape=jax.ShapeDtype...]
    ppermute x8 -> x0, starting transfers between devices: 27.6 us -> none  [the longest x4 14.7 us: extended(): lax.ppermute(tail, axis, [(i, (i + 1) % count) for i in range(ends)])]
    all_to_all x2 -> x0, blocking collectives: 19.2 us -> none  [sent_to_all(): return lax.all_to_all(copies, axis, split_axis=0, concat_axis=0, tiled=True)]
    ppermute x8 -> x0, waiting for transfers between devices: 13.2 us -> none  [the longest x4 12 us: extended(): lax.ppermute(head, axis, [((i + 1) % count, i) for i in range(ends)])]
    dot_general x54 -> x0, matrix products: 12.8 us -> none  [conv_local(): jnp.dot(window, kernel[along_x, along_y, along_z], preferred_element_type...]
    slice x5 -> x0, local copies, waits for them, and re-layouts: 4.97 us -> none  [the longest x3 3.95 us: conv_local(): padded[along_x:along_x + extent_x, along_y:along_y + extent_y, along_z:al...]
    unnamed x7 -> x6, local copies, waits for them, and re-layouts: 0.26 us -> 3.39 us
    concatenate x4 -> x0, other arithmetic: 2.42 us -> none  [extended(): jnp.concatenate([lax.ppermute(tail, axis, [(i, (i + 1) % count) for i in...]
  transfers between devices with their start and end apart: 8 -> 0, of which waited for: 5 -> 0; matrix products, arithmetic and copies ran while one was open for 1% -> 0% of each run, Pallas kernels for 0% -> 0%
where the time goes in v1:
time: 37 us; the launch traced here: 36.8 us
  Pallas kernels  32.5 us (88%)
  local copies, waits for them, and re-layouts  4.3 us (12%)
    pallas_call x1, Pallas kernels, body(): pl.pallas_call(functools.partial(kernel, sizes), out_shape=jax.ShapeDtype...  32.5 us
    unnamed x6, local copies, waits for them, and re-layouts  3.39 us
    transpose x1, local copies, waits for them, and re-layouts, body(): cells = packed.reshape(4, 2, PLANE, 4, FILTERS).transpose(0, 3, 1, 2, 4)  0.75 us

profile of v1, /device:TPU:1, one launch (start us, length us, event | category | flops | bytes accessed | tf_op | source)
XLA Modules:
  0.0 36.8 jit_solution(15986778320729799303)
XLA Ops:
  0.0 0.0 copy-start
  0.0 1.5 %copy-done = bf16[3,3,3,128,256]{4,3,2,1,0:T(8,128)(2,1)S(1)} copy-done((bf16[3,3,3,128,256]{4,3,2,1,0:T(8,128)(2,1)S(1)}, bf16[3,3,3,128,256]{4,3,2,1,0:T(8,128)(2,1)}, u32[]{:S(2)}) %copy-start) | copy-done | bytes 1769496
  1.5 0.0 copy-start.1
  1.5 1.0 %copy-done.1 = bf16[3,3,3,256,32]{3,4,2,1,0:T(8,128)(2,1)S(1)} copy-done((bf16[3,3,3,256,32]{3,4,2,1,0:T(8,128)(2,1)S(1)}, bf16[3,3,3,256,32]{3,4,2,1,0:T(8,128)(2,1)}, u32[]{:S(2)}) %copy-start.1) | copy-done | bytes 442392
  2.5 0.0 copy-start.2
  2.5 0.9 %copy-done.2 = bf16[2,16,16,128]{3,2,1,0:T(8,128)(2,1)S(1)} copy-done((bf16[2,16,16,128]{3,2,1,0:T(8,128)(2,1)S(1)}, bf16[2,16,16,128]{3,2,1,0:T(8,128)(2,1)}, u32[]{:S(2)}) %copy-start.2) | copy-done | bytes 131096
  3.4 32.5 %shard_map.37 = bf16[4,64,128]{2,1,0:T(8,128)(2,1)S(1)} custom-call(bf16[2,16,16,128]{3,2,1,0:T(8,128)(2,1)S(1)} %copy-done.2, bf16[3456,256]{1,0:T(8,128)(2,1)S(1)} %bitcast.4, bf16[3,3,3,32,256]{4,3,2,1,0:T(8,128)(2,1)S(1)} %bitcast.5), custom_call_target="tpu_custom_call" | custom-call | tf_op jit(solution)/shard_map/pallas_call | solution.py:285
  35.9 0.2 reshape.10
  36.0 0.8 %copy.4 = bf16[4,4,2,32,32]{4,3,2,1,0:T(8,128)(2,1)} copy(bf16[4,4,2,32,32]{4,1,3,2,0:T(4,128)(2,1)S(1)} %bitcast.6) | data formatting | bytes 131072 | tf_op jit(solution)/shard_map/transpose | solution.py:324
Async XLA Ops:
  0.0 1.5 %copy-start = (bf16[3,3,3,128,256]{4,3,2,1,0:T(8,128)(2,1)S(1)}, bf16[3,3,3,128,256]{4,3,2,1,0:T(8,128)(2,1)}, u32[]{:S(2)}) copy-start(bf16[3,3,3,128,256]{4,3,2,1,0:T(8,128)(2,1)} %param.4) | copy-start | bytes 5308420
  1.5 1.0 %copy-start.1 = (bf16[3,3,3,256,32]{3,4,2,1,0:T(8,128)(2,1)S(1)}, bf16[3,3,3,256,32]{3,4,2,1,0:T(8,128)(2,1)}, u32[]{:S(2)}) copy-start(bf16[3,3,3,256,32]{3,4,2,1,0:T(8,128)(2,1)} %param.5) | copy-start | bytes 1327108
  2.5 0.9 %copy-start.2 = (bf16[2,16,16,128]{3,2,1,0:T(8,128)(2,1)S(1)}, bf16[2,16,16,128]{3,2,1,0:T(8,128)(2,1)}, u32[]{:S(2)}) copy-start(bf16[2,16,16,128]{3,2,1,0:T(8,128)(2,1)} %v.1) | copy-start | bytes 393220

commit v2 on v1

--- a/solution.py
+++ b/solution.py
@@ -16,11 +16,15 @@
 
 def kernel(
     sizes, v, w4, w5, out,
-    pad, wide, taps, w4b, w5b, zs, yz, zh, ch, pool, block, blocks, slab, edge, sent, got, packed,
-    load_sem, halo_send, halo_recv, block_send, block_recv, part_send, part_recv,
+    pad, wide, taps, w4b, w5b, zs, yz, zh, ch, pool, block, blocks, rim, rims, slab, edge, sent, got, packed,
+    load_sem, halo_send, halo_recv, block_send, block_recv, rim_send, rim_recv, part_send, part_recv, shard_send, shard_recv,
 ):
     ngx, ngy, ngz = sizes
     g, a, b = lax.axis_index("gx"), lax.axis_index("gy"), lax.axis_index("gz")
+    half = lax.div(a, 2)
+    core = lax.rem(g, 2)
+    other = ngy - 1 - a
+    beside = 4 * half + 1 - a
 
     def there(dg, da, db):
         ok = None
@@ -50,6 +54,38 @@
     for load in w5_loads:
         load.start()
 
+    def finish(stage):
+        if stage < 3:
+            w4_load.wait()
+        if stage < 2:
+            for load in w5_loads:
+                load.wait()
+        if stage >= 2:
+            for shift in SHIFTS:
+                @pl.when(there(*shift))
+                def _():
+                    halo(shift).wait_send()
+        if stage >= 2:
+            shard_copy().wait_send()
+            if stage < 4:
+                shard_copy().wait_recv()
+        if stage >= 4:
+            shard_relay().wait_send()
+            for di, db in offsets:
+                spread(di, db).wait_send()
+
+            @pl.when(jnp.logical_or(a == 1, a == 2))
+            def _():
+                for t in range(2):
+                    for db in range(ngz):
+                        rim_copy(t, db).wait_send()
+        if stage >= 5:
+            for p, k in parts:
+                @part_when(k, True)
+                def _():
+                    for q in range(2):
+                        part_copy(p, k, q).wait_send()
+
     barrier = pltpu.get_barrier_semaphore()
     for da in range(ngy):
         for db in range(ngz):
@@ -63,10 +99,16 @@
             def _():
                 pl.semaphore_signal(barrier, inc=1, device_id=device(*shift), device_id_type=MESH)
 
+    outer = jnp.logical_or(a == 0, a == ngy - 1)
+    for dg in (-1, 1):
+        @pl.when(jnp.logical_and(there(dg, 0, 0), outer))
+        def _():
+            pl.semaphore_signal(barrier, inc=1, device_id={"gx": g + dg, "gy": other}, device_id_type=MESH)
+
     def near(at, n):
         return jnp.int32(1) + (at > 0).astype(jnp.int32) + (at < n - 1).astype(jnp.int32)
 
-    greeted = (near(g, ngx) - 1) * near(a, ngy) * near(b, ngz) + (ngy * ngz - 1)
+    greeted = (near(g, ngx) - 1) * (near(a, ngy) * near(b, ngz) + outer.astype(jnp.int32)) + (ngy * ngz - 1)
 
     @pl.when(g == 0)
     def _():
@@ -92,11 +134,10 @@
             zh[side] = jnp.zeros((4, 16, CIN), BF16)
             ch[side] = jnp.zeros((2, 3, 8, CIN), F32)
 
-    slab[0] = jnp.zeros((PLANE, C4), BF16)
-    slab[PLANE + 1] = jnp.zeros((PLANE, C4), BF16)
-    w5b[:, 96:128, :] = jnp.zeros((3, 32, 3 * C4), BF16)
-    edge[:, :, 0:8] = jnp.zeros((2, 8, 8, 128), F32)
-    edge[:, :, 40:48] = jnp.zeros((2, 8, 8, 128), F32)
+    slab[17 * half] = jnp.zeros((PLANE, C4), BF16)
+    w5b[:, 192:256, :] = jnp.zeros((3, 64, 3 * C4), BF16)
+    edge[:, :, 0:8] = jnp.zeros((2, 8, 8, 256), F32)
+    edge[:, :, 40:48] = jnp.zeros((2, 8, 8, 256), F32)
     yz[...] = jnp.zeros(yz.shape, F32)
 
     own_load.wait()
@@ -146,6 +187,26 @@
         @pl.when(there(*shift))
         def _():
             halo(shift).start()
+
+    def shard_rows(first, which):
+        return w5b.at[:, pl.ds(pl.multiple_of(first + 48 * which, 16), 48), :]
+
+    def shard_copy():
+        return pltpu.make_async_remote_copy(
+            src_ref=shard_rows(0, core), dst_ref=shard_rows(96, core), send_sem=shard_send.at[0], recv_sem=shard_recv.at[0],
+            device_id={"gy": other}, device_id_type=MESH,
+        )
+
+    def shard_relay():
+        return pltpu.make_async_remote_copy(
+            src_ref=shard_rows(96, core), dst_ref=shard_rows(96, core), send_sem=shard_send.at[1], recv_sem=shard_recv.at[1],
+            device_id={"gx": g + 1 - 2 * core}, device_id_type=MESH,
+        )
+
+    for load in w5_loads:
+        load.wait()
+    shard_copy().start()
+
     for shift in SHIFTS:
         @pl.when(there(*(-i for i in shift)))
         def _():
@@ -179,104 +240,117 @@
             hidden = jnp.dot(lhs, w4b[...], preferred_element_type=F32)
             tops = hidden if tops is None else jnp.maximum(tops, hidden)
         tops = jnp.max(tops.reshape(2, 2, 16, C4), axis=1).reshape(32, C4)
-        for half in range(2):
-            pool[half, part * 32 : part * 32 + 32, :] = tops[:, half * 128 : half * 128 + 128]
-    for half in range(2):
-        tops = jnp.maximum(pool[half, pl.ds(0, 64, stride=2), :], pool[half, pl.ds(1, 64, stride=2), :])
-        block[:, half * 128 : half * 128 + 128] = jnp.where(tops > 0, tops, 0.3 * tops).astype(BF16)
-
-    me = a * ngz + b
-    offsets = [(da, db) for da in range(ngy) for db in range(ngz) if (da, db) != (0, 0)]
-
-    def spread(da, db):
-        number = da * ngz + db
-        return pltpu.make_async_remote_copy(
-            src_ref=block, dst_ref=blocks.at[me], send_sem=block_send.at[number], recv_sem=block_recv.at[number],
-            device_id={"gy": lax.rem(a + da, ngy), "gz": lax.rem(b + db, ngz)}, device_id_type=MESH,
-        )
-
-    for da, db in offsets:
-        spread(da, db).start()
-    blocks[me] = block[...]
-    for load in w5_loads:
-        load.wait()
-    for da, db in offsets:
-        spread(da, db).wait_recv()
-
-    for row in range(ngy):
+        for lanes in range(2):
+            pool[lanes, part * 32 : part * 32 + 32, :] = tops[:, lanes * 128 : lanes * 128 + 128]
+    for lanes in range(2):
+        tops = jnp.maximum(pool[lanes, pl.ds(0, 64, stride=2), :], pool[lanes, pl.ds(1, 64, stride=2), :])
+        block[:, lanes * 128 : lanes * 128 + 128] = jnp.where(tops > 0, tops, 0.3 * tops).astype(BF16)
+
+    mine = (a - 2 * half) * ngz + b
+    offsets = [(di, db) for di in range(2) for db in range(ngz) if (di, db) != (0, 0)]
+
+    def spread(di, db):
+        number = di * ngz + db
+        return pltpu.make_async_remote_copy(
+            src_ref=block, dst_ref=blocks.at[mine], send_sem=block_send.at[number], recv_sem=block_recv.at[number],
+            device_id={"gy": beside if di else a, "gz": lax.rem(b + db, ngz)}, device_id_type=MESH,
+        )
+
+    def rim_copy(t, db):
+        return pltpu.make_async_remote_copy(
+            src_ref=rim, dst_ref=rims.at[b], send_sem=rim_send.at[t, db], recv_sem=rim_recv.at[db],
+            device_id={"gy": 2 * (1 - half) + t, "gz": lax.rem(b + db, ngz)}, device_id_type=MESH,
+        )
+
+    for at, first in ((1, 56), (2, 0)):
+        @pl.when(a == at)
+        def _():
+            rim[...] = block[first : first + 8, :].astype(F32)
+
+    for di, db in offsets:
+        spread(di, db).start()
+
+    @pl.when(jnp.logical_or(a == 1, a == 2))
+    def _():
+        for t in range(2):
+            for db in range(ngz):
+                rim_copy(t, db).start()
+
+    blocks[mine] = block[...]
+    shard_copy().wait_recv()
+    shard_relay().start()
+    for di, db in offsets:
+        spread(di, db).wait_recv()
+    for db in range(ngz):
+        rim_copy(0, db).wait_recv()
+    shard_relay().wait_recv()
+
+    for row in range(2):
         for pair in range(2):
             halves = [blocks[row * ngz + 2 * pair + i].astype(F32).reshape(8, 1, 8, C4) for i in range(2)]
             tile = jnp.concatenate(halves, axis=1).reshape(8, 16, C4).astype(BF16)
             slab[1 + 8 * row : 9 + 8 * row, 16 * pair : 16 * pair + 16, :] = tile
-
-    def part_copy(q, k):
-        dg = 1 if k == 0 else -1
-        return pltpu.make_async_remote_copy(
-            src_ref=sent.at[k, q], dst_ref=got.at[k, q], send_sem=part_send.at[k, q], recv_sem=part_recv.at[k, q],
-            device_id={"gx": g + dg}, device_id_type=MESH,
+    slab[17 * (1 - half)] = rims[...].reshape(PLANE, C4).astype(BF16)
+
+    parts = [(p, k) for p in range(2) for k in range(3) if (p, k) != (0, 1)]
+
+    def part_when(k, sender):
+        if k == 1:
+            return lambda f: f()
+        if (k == 0) == sender:
+            return pl.when(g < ngx - 1)
+        return pl.when(g > 0)
+
+    def part_copy(p, k, q):
+        return pltpu.make_async_remote_copy(
+            src_ref=sent.at[p, k, q], dst_ref=got.at[p, k, q], send_sem=part_send.at[p, k, q], recv_sem=part_recv.at[p, k, q],
+            device_id={"gx": g + 1 - k, "gy": other if p else a}, device_id_type=MESH,
         )
 
     lane = lax.broadcasted_iota(jnp.int32, (64, 128), 1)
 
-    def group(rows, k):
+    def group(rows, j):
+        tile, k = divmod(j, 4)
         moved = [
-            rows[64 * u : 64 * u + 64] if u == k else pltpu.roll(rows[64 * u : 64 * u + 64], (32 * (u - k)) % 128, axis=1)
+            pltpu.roll(rows[64 * u : 64 * u + 64, 128 * tile : 128 * tile + 128], (32 * (u - k)) % 128, axis=1)
+            if u != k else rows[64 * u : 64 * u + 64, 128 * tile : 128 * tile + 128]
             for u in range(4)
         ]
         return jnp.where(lane < 64, jnp.where(lane < 32, moved[0], moved[1]), jnp.where(lane < 96, moved[2], moved[3]))
 
-    for q in range(4):
+    for q in range(2):
         lhs = jnp.concatenate([slab[8 * q + dy : 8 * q + dy + 8].reshape(256, C4) for dy in range(3)], axis=-1)
         sums = [
-            lax.dot_general(lhs, w5b[dz], (((1,), (1,)), ((), ())), preferred_element_type=F32).reshape(8, PLANE, 128)
+            lax.dot_general(lhs, w5b[dz], (((1,), (1,)), ((), ())), preferred_element_type=F32).reshape(8, PLANE, 256)
             for dz in range(3)
         ]
         edge[0, :, 8:40] = sums[0]
         edge[1, :, 8:40] = sums[2]
-        total = (sums[1] + edge[0, :, 7:39] + edge[1, :, 9:41]).reshape(256, 128)
-        sent[0, q] = group(total, 0).astype(BF16)
-        sent[1, q] = group(total, 2).astype(BF16)
-
-        @pl.when(g < ngx - 1)
-        def _():
-            part_copy(q, 0).start()
-
-        @pl.when(g > 0)
-        def _():
-            part_copy(q, 1).start()
-
-        packed[q] = group(total, 1)
-
-    @pl.when(g > 0)
-    def _():
-        for q in range(4):
-            part_copy(q, 0).wait_recv()
-            packed[q] += got[0, q].astype(F32)
-
-    @pl.when(g < ngx - 1)
-    def _():
-        for q in range(4):
-            part_copy(q, 1).wait_recv()
-            packed[q] += got[1, q].astype(F32)
-
-    out[...] = packed[...].astype(BF16)
-
-    for shift in SHIFTS:
-        @pl.when(there(*shift))
-        def _():
-            halo(shift).wait_send()
-    for da, db in offsets:
-        spread(da, db).wait_send()
-
-    @pl.when(g < ngx - 1)
-    def _():
-        for q in range(4):
-            part_copy(q, 0).wait_send()
-
-    @pl.when(g > 0)
-    def _():
-        for q in range(4):
-            part_copy(q, 1).wait_send()
+        total = (sums[1] + edge[0, :, 7:39] + edge[1, :, 9:41]).reshape(256, 256)
+        for p, k in parts:
+            sent[p, k, q] = group(total, 3 * p + k).astype(BF16)
+
+            @part_when(k, True)
+            def _():
+                part_copy(p, k, q).start()
+
+        packed[0, q] = group(total, 1)
+
+    for q in range(2):
+        part_copy(1, 1, q).wait_recv()
+        packed[1, q] = got[1, 1, q].astype(F32)
+    for k in (0, 2):
+        @part_when(k, False)
+        def _():
+            for p in range(2):
+                for q in range(2):
+                    part_copy(p, k, q).wait_recv()
+                    packed[p, q] += got[p, k, q].astype(F32)
+
+    out[half] = packed[0].astype(BF16)
+    out[1 - half] = packed[1].astype(BF16)
+
+    finish(9)
 
 
 def body(sizes, volume, conv4_weight, conv5_weight):
@@ -284,7 +358,7 @@
     any_space = pl.BlockSpec(memory_space=pl.ANY)
     packed = pl.pallas_call(
         functools.partial(kernel, sizes),
-        out_shape=jax.ShapeDtypeStruct((4, 64, 128), BF16),
+        out_shape=jax.ShapeDtypeStruct((2, 2, 64, 128), BF16),
         in_specs=[any_space] * 3,
         out_specs=pl.BlockSpec(memory_space=pltpu.VMEM),
         scratch_shapes=[
@@ -292,34 +366,38 @@
             pltpu.VMEM((4 * 18 * 32, CIN), F32),
             pltpu.VMEM((4, 18 * 16, 3 * CIN), BF16),
             pltpu.VMEM((27 * CIN, C4), BF16),
-            pltpu.VMEM((3, 128, 3 * C4), BF16),
+            pltpu.VMEM((3, 256, 3 * C4), BF16),
             pltpu.VMEM((2, 2, 16, CIN), BF16),
             pltpu.VMEM((2, 2, 8, CIN), F32),
             pltpu.VMEM((2, 4, 16, CIN), BF16),
             pltpu.VMEM((2, 2, 3, 8, CIN), F32),
             pltpu.VMEM((2, 128, 128), F32),
             pltpu.VMEM((64, C4), BF16),
-            pltpu.VMEM((ngy * ngz, 64, C4), BF16),
-            pltpu.VMEM((PLANE + 2, PLANE, C4), BF16),
-            pltpu.VMEM((2, 8, 48, 128), F32),
-            pltpu.VMEM((2, 4, 64, 128), BF16),
-            pltpu.VMEM((2, 4, 64, 128), BF16),
-            pltpu.VMEM((4, 64, 128), F32),
+            pltpu.VMEM((2 * ngz, 64, C4), BF16),
+            pltpu.VMEM((8, C4), F32),
+            pltpu.VMEM((ngz, 8, C4), F32),
+            pltpu.VMEM((18, PLANE, C4), BF16),
+            pltpu.VMEM((2, 8, 48, 256), F32),
+            pltpu.VMEM((2, 3, 2, 64, 128), BF16),
+            pltpu.VMEM((2, 3, 2, 64, 128), BF16),
+            pltpu.VMEM((2, 2, 64, 128), F32),
             pltpu.SemaphoreType.DMA((11,)),
             pltpu.SemaphoreType.DMA((26,)),
             pltpu.SemaphoreType.DMA((26,)),
-            pltpu.SemaphoreType.DMA((ngy * ngz,)),
-            pltpu.SemaphoreType.DMA((ngy * ngz,)),
-            pltpu.SemaphoreType.DMA((2, 4)),
-            pltpu.SemaphoreType.DMA((2, 4)),
+            pltpu.SemaphoreType.DMA((2 * ngz,)),
+            pltpu.SemaphoreType.DMA((2 * ngz,)),
+            pltpu.SemaphoreType.DMA((2, ngz)),
+            pltpu.SemaphoreType.DMA((ngz,)),
+            pltpu.SemaphoreType.DMA((2, 3, 2)),
+            pltpu.SemaphoreType.DMA((2, 3, 2)),
+            pltpu.SemaphoreType.DMA((2,)),
+            pltpu.SemaphoreType.DMA((2,)),
         ],
         compiler_params=pltpu.CompilerParams(
             collective_id=0, has_side_effects=True, vmem_limit_bytes=40 * 1024 * 1024
         ),
     )(
-        volume,
-        conv4_weight.reshape(27 * CIN, C4),
-        jnp.swapaxes(conv5_weight, 3, 4),
+        *(pltpu.with_memory_space_constraint(x, pltpu.HBM) for x in (volume, conv4_weight.reshape(27 * CIN, C4), jnp.swapaxes(conv5_weight, 3, 4))),
     )
     cells = packed.reshape(4, 2, PLANE, 4, FILTERS).transpose(0, 3, 1, 2, 4)
     return cells.reshape(1, PLANE, PLANE, FILTERS)

time: 37 us -> 30.5 us (0.82)
  local copies, waits for them, and re-layouts: 4.3 us -> 0.9 us
  Pallas kernels: 32.5 us -> 29.5 us
    unnamed x6 -> x0, local copies, waits for them, and re-layouts: 3.39 us -> none
    pallas_call x1, Pallas kernels: 32.5 us -> 29.5 us  [body(): pl.pallas_call(functools.partial(kernel, sizes), out_shape=jax.ShapeDtype...]
where the time goes in v2:
time: 30.5 us; the launch traced here: 30.4 us
  Pallas kernels  29.5 us (97%)
  local copies, waits for them, and re-layouts  0.9 us (3%)
    pallas_call x1, Pallas kernels, body(): pl.pallas_call(functools.partial(kernel, sizes), out_shape=jax.ShapeDtype...  29.5 us
    transpose x1, local copies, waits for them, and re-layouts, body(): cells = packed.reshape(4, 2, PLANE, 4, FILTERS).transpose(0, 3, 1, 2, 4)  0.75 us

profile of v2, /device:TPU:1, one launch (start us, length us, event | category | flops | bytes accessed | tf_op | source)
XLA Modules:
  0.0 30.4 jit_solution(11302379366749016822)
XLA Ops:
  0.0 29.5 %shard_map.37 = bf16[2,2,64,128]{3,2,1,0:T(8,128)(2,1)S(1)} custom-call(bf16[2,16,16,128]{3,2,1,0:T(8,128)(2,1)} %v.1, bf16[3456,256]{1,0:T(8,128)(2,1)} %bitcast.6, bf16[3,3,3,32,256]{4,3,2,1,0:T(8,128)(2,1)} %bitcast.8), custom_call_target="tpu_custom_call" | custom-call | tf_op jit(solution)/shard_map/pallas_call | solution.py:359
  29.5 0.2 reshape.10
  29.6 0.8 %copy.4 = bf16[4,4,2,32,32]{4,3,2,1,0:T(8,128)(2,1)} copy(bf16[4,4,2,32,32]{4,1,3,2,0:T(4,128)(2,1)S(1)} %bitcast.7) | data formatting | bytes 131072 | tf_op jit(solution)/shard_map/transpose | solution.py:402

commit v3 on v2

--- a/solution.py
+++ b/solution.py
@@ -16,7 +16,7 @@
 
 def kernel(
     sizes, v, w4, w5, out,
-    pad, wide, taps, w4b, w5b, zs, yz, zh, ch, pool, block, blocks, rim, rims, slab, edge, sent, got, packed,
+    pad, wide, taps, w4b, w5b, zs, yz, zh, ch, hidden, pool, block, blocks, rim, rims, slab, broad, sent, got, packed,
     load_sem, halo_send, halo_recv, block_send, block_recv, rim_send, rim_recv, part_send, part_recv, shard_send, shard_recv,
 ):
     ngx, ngy, ngz = sizes
@@ -37,48 +37,54 @@
     def device(dg, da, db):
         return {"gx": g + dg, "gy": a + da, "gz": b + db}
 
+    barrier = pltpu.get_barrier_semaphore()
+    ring = sorted(SHIFTS, key=lambda shift: -sum(map(abs, shift)))
+    for dg, da, db in ring:
+        def greet():
+            pl.semaphore_signal(
+                barrier, inc=1,
+                device_id={"gx": g + dg, "gy": lax.rem(a + da + ngy, ngy), "gz": lax.rem(b + db + ngz, ngz)},
+                device_id_type=MESH,
+            )
+        if dg:
+            pl.when(there(dg, 0, 0))(greet)
+        else:
+            greet()
+    sides = (g > 0).astype(jnp.int32) + (g < ngx - 1).astype(jnp.int32)
+    greeted = 9 * sides + 8
+
     own_load = pltpu.make_async_copy(v, pad.at[1:3, 1:17], load_sem.at[0])
     own_load.start()
     w4_load = pltpu.make_async_copy(w4, w4b, load_sem.at[1])
     w4_load.start()
-    w5_loads = []
-    for dx in range(3):
-        for dy in range(3):
-            w5_loads.append(
-                pltpu.make_async_copy(
-                    w5.at[dx, dy],
-                    w5b.at[:, dx * FILTERS : (dx + 1) * FILTERS, dy * C4 : (dy + 1) * C4],
-                    load_sem.at[2 + dx * 3 + dy],
-                )
-            )
+    w5_loads = [
+        pltpu.make_async_copy(
+            w5.at[dx, dy, dz],
+            w5b.at[dx * FILTERS : (dx + 1) * FILTERS, (3 * dz + dy) * C4 : (3 * dz + dy + 1) * C4],
+            load_sem.at[2 + (dx * 3 + dy) * 3 + dz],
+        )
+        for dx in range(3)
+        for dy in range(3)
+        for dz in range(3)
+    ]
     for load in w5_loads:
         load.start()
 
     def finish(stage):
-        if stage < 3:
+        if stage < 2:
             w4_load.wait()
         if stage < 2:
             for load in w5_loads:
                 load.wait()
-        if stage >= 2:
-            for shift in SHIFTS:
-                @pl.when(there(*shift))
-                def _():
-                    halo(shift).wait_send()
-        if stage >= 2:
+        if stage == 2:
+            halo_wait([shift for shift in SHIFTS if shift[0]])
+            w4_load.wait()
+        if 2 <= stage < 4:
+            halo_sent()
             shard_copy().wait_send()
-            if stage < 4:
-                shard_copy().wait_recv()
-        if stage >= 4:
-            shard_relay().wait_send()
-            for di, db in offsets:
-                spread(di, db).wait_send()
-
-            @pl.when(jnp.logical_or(a == 1, a == 2))
-            def _():
-                for t in range(2):
-                    for db in range(ngz):
-                        rim_copy(t, db).wait_send()
+            shard_copy().wait_recv()
+        if stage == 4:
+            spread_sent()
         if stage >= 5:
             for p, k in parts:
                 @part_when(k, True)
@@ -86,30 +92,6 @@
                     for q in range(2):
                         part_copy(p, k, q).wait_send()
 
-    barrier = pltpu.get_barrier_semaphore()
-    for da in range(ngy):
-        for db in range(ngz):
-            if (da, db) != (0, 0):
-                pl.semaphore_signal(
-                    barrier, inc=1, device_id={"gy": lax.rem(a + da, ngy), "gz": lax.rem(b + db, ngz)}, device_id_type=MESH
-                )
-    for shift in SHIFTS:
-        if shift[0]:
-            @pl.when(there(*shift))
-            def _():
-                pl.semaphore_signal(barrier, inc=1, device_id=device(*shift), device_id_type=MESH)
-
-    outer = jnp.logical_or(a == 0, a == ngy - 1)
-    for dg in (-1, 1):
-        @pl.when(jnp.logical_and(there(dg, 0, 0), outer))
-        def _():
-            pl.semaphore_signal(barrier, inc=1, device_id={"gx": g + dg, "gy": other}, device_id_type=MESH)
-
-    def near(at, n):
-        return jnp.int32(1) + (at > 0).astype(jnp.int32) + (at < n - 1).astype(jnp.int32)
-
-    greeted = (near(g, ngx) - 1) * (near(a, ngy) * near(b, ngz) + outer.astype(jnp.int32)) + (ngy * ngz - 1)
-
     @pl.when(g == 0)
     def _():
         pad[0] = jnp.zeros(pad.shape[1:], BF16)
@@ -134,10 +116,11 @@
             zh[side] = jnp.zeros((4, 16, CIN), BF16)
             ch[side] = jnp.zeros((2, 3, 8, CIN), F32)
 
-    slab[17 * half] = jnp.zeros((PLANE, C4), BF16)
-    w5b[:, 192:256, :] = jnp.zeros((3, 64, 3 * C4), BF16)
-    edge[:, :, 0:8] = jnp.zeros((2, 8, 8, 256), F32)
-    edge[:, :, 40:48] = jnp.zeros((2, 8, 8, 256), F32)
+    for dz in range(3):
+        slab[dz, 17 * half] = jnp.zeros((PLANE, C4), BF16)
+    w5b[192:256, :] = jnp.zeros((64, 9 * C4), BF16)
+    broad[:, 0:8] = jnp.zeros((18, 8, C4), F32)
+    broad[:, 40:48] = jnp.zeros((18, 8, C4), F32)
     yz[...] = jnp.zeros(yz.shape, F32)
 
     own_load.wait()
@@ -183,13 +166,25 @@
             device_id=device(*shift), device_id_type=MESH,
         )
 
-    for shift in SHIFTS:
+    def halo_sent():
+        for shift in SHIFTS:
+            @pl.when(there(*shift))
+            def _():
+                halo(shift).wait_send()
+
+    def halo_wait(shifts):
+        for shift in shifts:
+            @pl.when(there(*(-i for i in shift)))
+            def _():
+                halo(shift).wait_recv()
+
+    for shift in ring:
         @pl.when(there(*shift))
         def _():
             halo(shift).start()
 
     def shard_rows(first, which):
-        return w5b.at[:, pl.ds(pl.multiple_of(first + 48 * which, 16), 48), :]
+        return w5b.at[pl.ds(pl.multiple_of(first + 48 * which, 16), 48), :]
 
     def shard_copy():
         return pltpu.make_async_remote_copy(
@@ -207,12 +202,7 @@
         load.wait()
     shard_copy().start()
 
-    for shift in SHIFTS:
-        @pl.when(there(*(-i for i in shift)))
-        def _():
-            halo(shift).wait_recv()
-
-    for x in range(4):
+    def widen(x):
         for y in range(18):
             if not (x in (1, 2) and 1 <= y <= 16):
                 row = (x * 18 + y) * 32 + 8
@@ -223,25 +213,34 @@
                 source, row = ((0, 1), (1, 0), (1, 1), (2, 0))[x]
                 first = (x * 18 + y) * 32 + at
                 wide[first : first + 1, :] = ch[side, ys, source, row : row + 1, :]
-    for x in range(4):
         for y in range(18):
             row = (x * 18 + y) * 32
             left = wide[row + 7 : row + 23, :].astype(BF16)
             right = wide[row + 9 : row + 25, :].astype(BF16)
             taps[x, y * 16 : y * 16 + 16, :] = jnp.concatenate([left, pad[x, y], right], axis=-1)
 
+    def around(x):
+        return jnp.concatenate([taps[x, dy * 16 : dy * 16 + 256, :] for dy in range(3)], axis=-1)
+
+    halo_wait([shift for shift in SHIFTS if shift[0] == 0])
+    for x in (1, 2):
+        widen(x)
     w4_load.wait()
-    for part in range(4):
-        tops = None
-        for x in (0, 1):
-            lhs = jnp.concatenate(
-                [taps[x + dx, (4 * part + dy) * 16 : (4 * part + dy) * 16 + 64, :] for dx in range(3) for dy in range(3)], axis=-1
-            )
-            hidden = jnp.dot(lhs, w4b[...], preferred_element_type=F32)
-            tops = hidden if tops is None else jnp.maximum(tops, hidden)
-        tops = jnp.max(tops.reshape(2, 2, 16, C4), axis=1).reshape(32, C4)
-        for lanes in range(2):
-            pool[lanes, part * 32 : part * 32 + 32, :] = tops[:, lanes * 128 : lanes * 128 + 128]
+    span = 9 * CIN
+    own = jnp.concatenate([around(1), around(2)], axis=-1)
+    for x in (0, 1):
+        first = (1 - x) * span
+        hidden[x] = jnp.dot(own, w4b[first : first + 2 * span, :], preferred_element_type=F32)
+    halo_wait([shift for shift in SHIFTS if shift[0]])
+    for x in (0, 3):
+        widen(x)
+    tops = jnp.maximum(
+        hidden[0] + jnp.dot(around(0), w4b[:span, :], preferred_element_type=F32),
+        hidden[1] + jnp.dot(around(3), w4b[2 * span :, :], preferred_element_type=F32),
+    )
+    tops = jnp.max(tops.reshape(8, 2, 16, C4), axis=1).reshape(128, C4)
+    for lanes in range(2):
+        pool[lanes] = tops[:, lanes * 128 : lanes * 128 + 128]
     for lanes in range(2):
         tops = jnp.maximum(pool[lanes, pl.ds(0, 64, stride=2), :], pool[lanes, pl.ds(1, 64, stride=2), :])
         block[:, lanes * 128 : lanes * 128 + 128] = jnp.where(tops > 0, tops, 0.3 * tops).astype(BF16)
@@ -277,22 +276,42 @@
                 rim_copy(t, db).start()
 
     blocks[mine] = block[...]
+    halo_sent()
     shard_copy().wait_recv()
     shard_relay().start()
-    for di, db in offsets:
-        spread(di, db).wait_recv()
+
+    def spread_sent():
+        shard_copy().wait_send()
+        shard_relay().wait_send()
+        for di, db in offsets:
+            spread(di, db).wait_send()
+
+        @pl.when(jnp.logical_or(a == 1, a == 2))
+        def _():
+            for t in range(2):
+                for db in range(ngz):
+                    rim_copy(t, db).wait_send()
+
+    def lay(first, rows):
+        for dz in range(3):
+            for row in range(rows):
+                slab[dz, first + row] = broad[first + row, 7 + dz : 39 + dz, :].astype(BF16)
+
+    for di, row in ((0, a - 2 * half), (1, 1 - a + 2 * half)):
+        for db in range(ngz):
+            if (di, db) != (0, 0):
+                spread(di, db).wait_recv()
+        for z in range(ngz):
+            broad[pl.ds(1 + 8 * row, 8), 8 + 8 * z : 16 + 8 * z, :] = blocks[row * ngz + z].astype(F32).reshape(8, 8, C4)
+        lay(1 + 8 * row, 8)
     for db in range(ngz):
         rim_copy(0, db).wait_recv()
+    for z in range(ngz):
+        broad[17 * (1 - half), 8 + 8 * z : 16 + 8 * z, :] = rims[z]
+    lay(17 * (1 - half), 1)
     shard_relay().wait_recv()
 
-    for row in range(2):
-        for pair in range(2):
-            halves = [blocks[row * ngz + 2 * pair + i].astype(F32).reshape(8, 1, 8, C4) for i in range(2)]
-            tile = jnp.concatenate(halves, axis=1).reshape(8, 16, C4).astype(BF16)
-            slab[1 + 8 * row : 9 + 8 * row, 16 * pair : 16 * pair + 16, :] = tile
-    slab[17 * (1 - half)] = rims[...].reshape(PLANE, C4).astype(BF16)
-
-    parts = [(p, k) for p in range(2) for k in range(3) if (p, k) != (0, 1)]
+    parts = [(p, k) for p in (1, 0) for k in (0, 2, 1) if (p, k) != (0, 1)]
 
     def part_when(k, sender):
         if k == 1:
@@ -318,24 +337,25 @@
         ]
         return jnp.where(lane < 64, jnp.where(lane < 32, moved[0], moved[1]), jnp.where(lane < 96, moved[2], moved[3]))
 
+    totals = []
     for q in range(2):
-        lhs = jnp.concatenate([slab[8 * q + dy : 8 * q + dy + 8].reshape(256, C4) for dy in range(3)], axis=-1)
-        sums = [
-            lax.dot_general(lhs, w5b[dz], (((1,), (1,)), ((), ())), preferred_element_type=F32).reshape(8, PLANE, 256)
-            for dz in range(3)
-        ]
-        edge[0, :, 8:40] = sums[0]
-        edge[1, :, 8:40] = sums[2]
-        total = (sums[1] + edge[0, :, 7:39] + edge[1, :, 9:41]).reshape(256, 256)
-        for p, k in parts:
-            sent[p, k, q] = group(total, 3 * p + k).astype(BF16)
-
-            @part_when(k, True)
-            def _():
+        lhs = jnp.concatenate(
+            [slab[dz, 8 * q + dy : 8 * q + dy + 8].reshape(256, C4) for dz in range(3) for dy in range(3)], axis=-1
+        )
+        totals.append(lax.dot_general(lhs, w5b[...], (((1,), (1,)), ((), ())), preferred_element_type=F32))
+    for p, k in parts:
+        for q in range(2):
+            sent[p, k, q] = group(totals[q], 3 * p + k).astype(BF16)
+
+        @part_when(k, True)
+        def _():
+            for q in range(2):
                 part_copy(p, k, q).start()
 
-        packed[0, q] = group(total, 1)
-
+    for q in range(2):
+        packed[0, q] = group(totals[q], 1)
+
+    spread_sent()
     for q in range(2):
         part_copy(1, 1, q).wait_recv()
         packed[1, q] = got[1, 1, q].astype(F32)
@@ -366,22 +386,23 @@
             pltpu.VMEM((4 * 18 * 32, CIN), F32),
             pltpu.VMEM((4, 18 * 16, 3 * CIN), BF16),
             pltpu.VMEM((27 * CIN, C4), BF16),
-            pltpu.VMEM((3, 256, 3 * C4), BF16),
+            pltpu.VMEM((256, 9 * C4), BF16),
             pltpu.VMEM((2, 2, 16, CIN), BF16),
             pltpu.VMEM((2, 2, 8, CIN), F32),
             pltpu.VMEM((2, 4, 16, CIN), BF16),
             pltpu.VMEM((2, 2, 3, 8, CIN), F32),
+            pltpu.VMEM((2, 256, C4), F32),
             pltpu.VMEM((2, 128, 128), F32),
             pltpu.VMEM((64, C4), BF16),
             pltpu.VMEM((2 * ngz, 64, C4), BF16),
             pltpu.VMEM((8, C4), F32),
             pltpu.VMEM((ngz, 8, C4), F32),
-            pltpu.VMEM((18, PLANE, C4), BF16),
-            pltpu.VMEM((2, 8, 48, 256), F32),
+            pltpu.VMEM((3, 18, PLANE, C4), BF16),
+            pltpu.VMEM((18, 48, C4), F32),
             pltpu.VMEM((2, 3, 2, 64, 128), BF16),
             pltpu.VMEM((2, 3, 2, 64, 128), BF16),
             pltpu.VMEM((2, 2, 64, 128), F32),
-            pltpu.SemaphoreType.DMA((11,)),
+            pltpu.SemaphoreType.DMA((29,)),
             pltpu.SemaphoreType.DMA((26,)),
             pltpu.SemaphoreType.DMA((26,)),
             pltpu.SemaphoreType.DMA((2 * ngz,)),

time: 30.5 us -> 27.5 us (0.902)
  Pallas kernels: 29.5 us -> 26.5 us
    pallas_call x1, Pallas kernels: 29.5 us -> 26.5 us  [body(): pl.pallas_call(functools.partial(kernel, sizes), out_shape=jax.ShapeDtype...]
where the time goes in v3:
time: 27.5 us; the launch traced here: 27.4 us
  Pallas kernels  26.5 us (96%)
  local copies, waits for them, and re-layouts  0.9 us (3%)
    pallas_call x1, Pallas kernels, body(): pl.pallas_call(functools.partial(kernel, sizes), out_shape=jax.ShapeDtype...  26.5 us
    transpose x1, local copies, waits for them, and re-layouts, body(): cells = packed.reshape(4, 2, PLANE, 4, FILTERS).transpose(0, 3, 1, 2, 4)  0.75 us

profile of v3, /device:TPU:1, one launch (start us, length us, event | category | flops | bytes accessed | tf_op | source)
XLA Modules:
  0.0 27.4 jit_solution(395914337000024909)
XLA Ops:
  0.0 26.5 %shard_map.37 = bf16[2,2,64,128]{3,2,1,0:T(8,128)(2,1)S(1)} custom-call(bf16[2,16,16,128]{3,2,1,0:T(8,128)(2,1)} %v.1, bf16[3456,256]{1,0:T(8,128)(2,1)} %bitcast.6, bf16[3,3,3,32,256]{4,3,2,1,0:T(8,128)(2,1)} %bitcast.8), custom_call_target="tpu_custom_call" | custom-call | tf_op jit(solution)/shard_map/pallas_call | solution.py:379
  26.5 0.2 reshape.10
  26.7 0.8 %copy.4 = bf16[4,4,2,32,32]{4,3,2,1,0:T(8,128)(2,1)} copy(bf16[4,4,2,32,32]{4,1,3,2,0:T(4,128)(2,1)S(1)} %bitcast.7) | data formatting | bytes 131072 | tf_op jit(solution)/shard_map/transpose | solution.py:423

commit v4 on v3

--- a/solution.py
+++ b/solution.py
@@ -16,7 +16,7 @@
 
 def kernel(
     sizes, v, w4, w5, out,
-    pad, wide, taps, w4b, w5b, zs, yz, zh, ch, hidden, pool, block, blocks, rim, rims, slab, broad, sent, got, packed,
+    pad, wide, taps, w4b, w5b, zs, yz, zh, ch, hidden, early, late, pool, block, blocks, rim, rims, slab, broad, sent, got, packed,
     load_sem, halo_send, halo_recv, block_send, block_recv, rim_send, rim_recv, part_send, part_recv, shard_send, shard_recv,
 ):
     ngx, ngy, ngz = sizes
@@ -37,38 +37,32 @@
     def device(dg, da, db):
         return {"gx": g + dg, "gy": a + da, "gz": b + db}
 
-    barrier = pltpu.get_barrier_semaphore()
-    ring = sorted(SHIFTS, key=lambda shift: -sum(map(abs, shift)))
-    for dg, da, db in ring:
-        def greet():
-            pl.semaphore_signal(
-                barrier, inc=1,
-                device_id={"gx": g + dg, "gy": lax.rem(a + da + ngy, ngy), "gz": lax.rem(b + db + ngz, ngz)},
-                device_id_type=MESH,
-            )
-        if dg:
-            pl.when(there(dg, 0, 0))(greet)
-        else:
-            greet()
-    sides = (g > 0).astype(jnp.int32) + (g < ngx - 1).astype(jnp.int32)
-    greeted = 9 * sides + 8
-
     own_load = pltpu.make_async_copy(v, pad.at[1:3, 1:17], load_sem.at[0])
     own_load.start()
     w4_load = pltpu.make_async_copy(w4, w4b, load_sem.at[1])
     w4_load.start()
     w5_loads = [
-        pltpu.make_async_copy(
-            w5.at[dx, dy, dz],
-            w5b.at[dx * FILTERS : (dx + 1) * FILTERS, (3 * dz + dy) * C4 : (3 * dz + dy + 1) * C4],
-            load_sem.at[2 + (dx * 3 + dy) * 3 + dz],
-        )
-        for dx in range(3)
-        for dy in range(3)
-        for dz in range(3)
+        pltpu.make_async_copy(w5.at[dx], w5b.at[:, dx * FILTERS : (dx + 1) * FILTERS, :], load_sem.at[2 + dx]) for dx in range(3)
     ]
     for load in w5_loads:
         load.start()
+
+    barrier = pltpu.get_barrier_semaphore()
+    near_a = {da: lax.rem(a + da + ngy, ngy) for da in (-1, 0, 1)}
+    near_b = {db: lax.rem(b + db + ngz, ngz) for db in (-1, 0, 1)}
+
+    def greet(dg):
+        for da, db in sorted(((i, j) for i in (-1, 0, 1) for j in (-1, 0, 1)), key=lambda at: -abs(at[0]) - abs(at[1])):
+            if (dg, da, db) != (0, 0, 0):
+                pl.semaphore_signal(
+                    barrier, inc=1, device_id={"gx": g + dg, "gy": near_a[da], "gz": near_b[db]}, device_id_type=MESH
+                )
+
+    pl.when(g < ngx - 1)(lambda: greet(1))
+    pl.when(g > 0)(lambda: greet(-1))
+    greet(0)
+    sides = (g > 0).astype(jnp.int32) + (g < ngx - 1).astype(jnp.int32)
+    greeted = 9 * sides + 8
 
     def finish(stage):
         if stage < 2:
@@ -81,8 +75,9 @@
             w4_load.wait()
         if 2 <= stage < 4:
             halo_sent()
-            shard_copy().wait_send()
-            shard_copy().wait_recv()
+            for piece in range(3):
+                shard_copy(piece).wait_send()
+                shard_copy(piece).wait_recv()
         if stage == 4:
             spread_sent()
         if stage >= 5:
@@ -92,37 +87,7 @@
                     for q in range(2):
                         part_copy(p, k, q).wait_send()
 
-    @pl.when(g == 0)
-    def _():
-        pad[0] = jnp.zeros(pad.shape[1:], BF16)
-        zh[:, 0] = jnp.zeros((2, 16, CIN), BF16)
-        ch[:, :, 0] = jnp.zeros((2, 2, 8, CIN), F32)
-
-    @pl.when(g == ngx - 1)
-    def _():
-        pad[3] = jnp.zeros(pad.shape[1:], BF16)
-        zh[:, 3] = jnp.zeros((2, 16, CIN), BF16)
-        ch[:, :, 2] = jnp.zeros((2, 2, 8, CIN), F32)
-
-    for side, edge_at in ((0, 0), (1, ngy - 1)):
-        @pl.when(a == edge_at)
-        def _():
-            pad[:, 17 * side] = jnp.zeros((4, 16, CIN), BF16)
-            ch[:, side] = jnp.zeros((2, 3, 8, CIN), F32)
-
-    for side, edge_at in ((0, 0), (1, ngz - 1)):
-        @pl.when(b == edge_at)
-        def _():
-            zh[side] = jnp.zeros((4, 16, CIN), BF16)
-            ch[side] = jnp.zeros((2, 3, 8, CIN), F32)
-
-    for dz in range(3):
-        slab[dz, 17 * half] = jnp.zeros((PLANE, C4), BF16)
-    w5b[192:256, :] = jnp.zeros((64, 9 * C4), BF16)
-    broad[:, 0:8] = jnp.zeros((18, 8, C4), F32)
-    broad[:, 40:48] = jnp.zeros((18, 8, C4), F32)
     yz[...] = jnp.zeros(yz.shape, F32)
-
     own_load.wait()
     for x in (1, 2):
         for y in range(1, 17):
@@ -178,29 +143,61 @@
             def _():
                 halo(shift).wait_recv()
 
-    for shift in ring:
+    for shift in sorted(SHIFTS, key=lambda shift: (shift[0] != 0, -sum(map(abs, shift)))):
         @pl.when(there(*shift))
         def _():
             halo(shift).start()
-
-    def shard_rows(first, which):
-        return w5b.at[pl.ds(pl.multiple_of(first + 48 * which, 16), 48), :]
-
-    def shard_copy():
-        return pltpu.make_async_remote_copy(
-            src_ref=shard_rows(0, core), dst_ref=shard_rows(96, core), send_sem=shard_send.at[0], recv_sem=shard_recv.at[0],
+    @pl.when(g == 0)
+    def _():
+        pad[0] = jnp.zeros(pad.shape[1:], BF16)
+        zh[:, 0] = jnp.zeros((2, 16, CIN), BF16)
+        ch[:, :, 0] = jnp.zeros((2, 2, 8, CIN), F32)
+
+    @pl.when(g == ngx - 1)
+    def _():
+        pad[3] = jnp.zeros(pad.shape[1:], BF16)
+        zh[:, 3] = jnp.zeros((2, 16, CIN), BF16)
+        ch[:, :, 2] = jnp.zeros((2, 2, 8, CIN), F32)
+
+    for side, edge_at in ((0, 0), (1, ngy - 1)):
+        @pl.when(a == edge_at)
+        def _():
+            pad[:, 17 * side] = jnp.zeros((4, 16, CIN), BF16)
+            ch[:, side] = jnp.zeros((2, 3, 8, CIN), F32)
+
+    for side, edge_at in ((0, 0), (1, ngz - 1)):
+        @pl.when(b == edge_at)
+        def _():
+            zh[side] = jnp.zeros((4, 16, CIN), BF16)
+            ch[side] = jnp.zeros((2, 3, 8, CIN), F32)
+
+    for dz in range(3):
+        slab[dz, 17 * half] = jnp.zeros((PLANE, C4), BF16)
+    broad[:, 0:8] = jnp.zeros((18, 8, C4), F32)
+    broad[:, 40:48] = jnp.zeros((18, 8, C4), F32)
+
+
+    def shard_rows(first, piece):
+        return w5b.at[3 * piece : 3 * piece + 3, pl.ds(pl.multiple_of(first + 48 * core, 16), 48), :]
+
+    def shard_copy(piece):
+        return pltpu.make_async_remote_copy(
+            src_ref=shard_rows(0, piece), dst_ref=shard_rows(96, piece),
+            send_sem=shard_send.at[0, piece], recv_sem=shard_recv.at[0, piece],
             device_id={"gy": other}, device_id_type=MESH,
         )
 
-    def shard_relay():
-        return pltpu.make_async_remote_copy(
-            src_ref=shard_rows(96, core), dst_ref=shard_rows(96, core), send_sem=shard_send.at[1], recv_sem=shard_recv.at[1],
+    def shard_relay(piece):
+        return pltpu.make_async_remote_copy(
+            src_ref=shard_rows(96, piece), dst_ref=shard_rows(96, piece),
+            send_sem=shard_send.at[1, piece], recv_sem=shard_recv.at[1, piece],
             device_id={"gx": g + 1 - 2 * core}, device_id_type=MESH,
         )
 
     for load in w5_loads:
         load.wait()
-    shard_copy().start()
+    for piece in range(3):
+        shard_copy(piece).start()
 
     def widen(x):
         for y in range(18):
@@ -264,25 +261,27 @@
     for at, first in ((1, 56), (2, 0)):
         @pl.when(a == at)
         def _():
-            rim[...] = block[first : first + 8, :].astype(F32)
-
-    for di, db in offsets:
-        spread(di, db).start()
+            rim[...] = block[first : first + 8, :]
 
     @pl.when(jnp.logical_or(a == 1, a == 2))
     def _():
-        for t in range(2):
-            for db in range(ngz):
+        for db in (2, 1, 3, 0):
+            for t in range(2):
                 rim_copy(t, db).start()
+
+    for di, db in ((1, 2), (0, 2), (1, 1), (1, 3), (0, 1), (0, 3), (1, 0)):
+        spread(di, db).start()
 
     blocks[mine] = block[...]
     halo_sent()
-    shard_copy().wait_recv()
-    shard_relay().start()
+    for piece in range(3):
+        shard_copy(piece).wait_recv()
+        shard_relay(piece).start()
 
     def spread_sent():
-        shard_copy().wait_send()
-        shard_relay().wait_send()
+        for piece in range(3):
+            shard_copy(piece).wait_send()
+            shard_relay(piece).wait_send()
         for di, db in offsets:
             spread(di, db).wait_send()
 
@@ -297,19 +296,41 @@
             for row in range(rows):
                 slab[dz, first + row] = broad[first + row, 7 + dz : 39 + dz, :].astype(BF16)
 
-    for di, row in ((0, a - 2 * half), (1, 1 - a + 2 * half)):
+    at = a - 2 * half
+    taps_w5 = (((1,), (1,)), ((), ()))
+
+    def settle(di, row):
         for db in range(ngz):
             if (di, db) != (0, 0):
                 spread(di, db).wait_recv()
         for z in range(ngz):
             broad[pl.ds(1 + 8 * row, 8), 8 + 8 * z : 16 + 8 * z, :] = blocks[row * ngz + z].astype(F32).reshape(8, 8, C4)
         lay(1 + 8 * row, 8)
+
+    def all_taps(numbers):
+        return jnp.concatenate([w5b[number] for number in numbers], axis=-1)
+
+    def rows_of(first, rows):
+        return jnp.concatenate(
+            [slab[dz, pl.ds(first + dy, rows)].reshape(rows * PLANE, C4) for dy in range(3) for dz in range(3)], axis=-1
+        )
+
+    settle(0, at)
+    for dz in range(3):
+        for row in (8 * at, 8 * at + 9):
+            slab[dz, row] = jnp.zeros((PLANE, C4), BF16)
+    for piece in range(3):
+        shard_relay(piece).wait_recv()
+    for part in range(2):
+        early[128 * part : 128 * part + 128, :192] = lax.dot_general(
+            rows_of(8 * at + 4 * part, 4), all_taps(range(9)), taps_w5, preferred_element_type=F32
+        )
+    settle(1, 1 - at)
     for db in range(ngz):
         rim_copy(0, db).wait_recv()
     for z in range(ngz):
-        broad[17 * (1 - half), 8 + 8 * z : 16 + 8 * z, :] = rims[z]
+        broad[17 * (1 - half), 8 + 8 * z : 16 + 8 * z, :] = rims[z].astype(F32)
     lay(17 * (1 - half), 1)
-    shard_relay().wait_recv()
 
     parts = [(p, k) for p in (1, 0) for k in (0, 2, 1) if (p, k) != (0, 1)]
 
@@ -337,38 +358,44 @@
         ]
         return jnp.where(lane < 64, jnp.where(lane < 32, moved[0], moved[1]), jnp.where(lane < 96, moved[2], moved[3]))
 
-    totals = []
-    for q in range(2):
-        lhs = jnp.concatenate(
-            [slab[dz, 8 * q + dy : 8 * q + dy + 8].reshape(256, C4) for dz in range(3) for dy in range(3)], axis=-1
-        )
-        totals.append(lax.dot_general(lhs, w5b[...], (((1,), (1,)), ((), ())), preferred_element_type=F32))
-    for p, k in parts:
-        for q in range(2):
-            sent[p, k, q] = group(totals[q], 3 * p + k).astype(BF16)
-
-        @part_when(k, True)
-        def _():
-            for q in range(2):
-                part_copy(p, k, q).start()
-
-    for q in range(2):
-        packed[0, q] = group(totals[q], 1)
+    def send_parts(total, slot):
+        for p, k in parts:
+            sent[p, k, slot] = group(total, 3 * p + k).astype(BF16)
+
+            @part_when(k, True)
+            def _():
+                part_copy(p, k, slot).start()
+
+        packed[0, slot] = group(total, 1)
+
+    for row, first, dy in ((8 * at, 0, 0), (8 * at + 9, 224, 2)):
+        early[first : first + PLANE, :192] += lax.dot_general(
+            jnp.concatenate([slab[dz, row] for dz in range(3)], axis=-1),
+            all_taps(range(3 * dy, 3 * dy + 3)),
+            taps_w5, preferred_element_type=F32,
+        )
+    send_parts(early[...], 0)
+    for part in range(2):
+        late[128 * part : 128 * part + 128, :192] = lax.dot_general(
+            rows_of(8 * (1 - at) + 4 * part, 4), all_taps(range(9)), taps_w5, preferred_element_type=F32
+        )
+    send_parts(late[...], 1)
 
     spread_sent()
-    for q in range(2):
-        part_copy(1, 1, q).wait_recv()
-        packed[1, q] = got[1, 1, q].astype(F32)
+    for slot in range(2):
+        part_copy(1, 1, slot).wait_recv()
+        packed[1, slot] = got[1, 1, slot].astype(F32)
     for k in (0, 2):
         @part_when(k, False)
         def _():
             for p in range(2):
-                for q in range(2):
-                    part_copy(p, k, q).wait_recv()
-                    packed[p, q] += got[p, k, q].astype(F32)
-
-    out[half] = packed[0].astype(BF16)
-    out[1 - half] = packed[1].astype(BF16)
+                for slot in range(2):
+                    part_copy(p, k, slot).wait_recv()
+                    packed[p, slot] += got[p, k, slot].astype(F32)
+
+    for p, place in ((0, half), (1, 1 - half)):
+        for slot in range(2):
+            out[place, at if p == slot else 1 - at] = packed[p, slot].astype(BF16)
 
     finish(9)
 
@@ -386,23 +413,25 @@
             pltpu.VMEM((4 * 18 * 32, CIN), F32),
             pltpu.VMEM((4, 18 * 16, 3 * CIN), BF16),
             pltpu.VMEM((27 * CIN, C4), BF16),
-            pltpu.VMEM((256, 9 * C4), BF16),
+            pltpu.VMEM((9, 192, C4), BF16),
             pltpu.VMEM((2, 2, 16, CIN), BF16),
             pltpu.VMEM((2, 2, 8, CIN), F32),
             pltpu.VMEM((2, 4, 16, CIN), BF16),
             pltpu.VMEM((2, 2, 3, 8, CIN), F32),
             pltpu.VMEM((2, 256, C4), F32),
+            pltpu.VMEM((256, 256), F32),
+            pltpu.VMEM((256, 256), F32),
             pltpu.VMEM((2, 128, 128), F32),
             pltpu.VMEM((64, C4), BF16),
             pltpu.VMEM((2 * ngz, 64, C4), BF16),
-            pltpu.VMEM((8, C4), F32),
-            pltpu.VMEM((ngz, 8, C4), F32),
+            pltpu.VMEM((8, C4), BF16),
+            pltpu.VMEM((ngz, 8, C4), BF16),
             pltpu.VMEM((3, 18, PLANE, C4), BF16),
             pltpu.VMEM((18, 48, C4), F32),
             pltpu.VMEM((2, 3, 2, 64, 128), BF16),
             pltpu.VMEM((2, 3, 2, 64, 128), BF16),
             pltpu.VMEM((2, 2, 64, 128), F32),
-            pltpu.SemaphoreType.DMA((29,)),
+            pltpu.SemaphoreType.DMA((5,)),
             pltpu.SemaphoreType.DMA((26,)),
             pltpu.SemaphoreType.DMA((26,)),
             pltpu.SemaphoreType.DMA((2 * ngz,)),
@@ -411,14 +440,14 @@
             pltpu.SemaphoreType.DMA((ngz,)),
             pltpu.SemaphoreType.DMA((2, 3, 2)),
             pltpu.SemaphoreType.DMA((2, 3, 2)),
-            pltpu.SemaphoreType.DMA((2,)),
-            pltpu.SemaphoreType.DMA((2,)),
+            pltpu.SemaphoreType.DMA((2, 3)),
+            pltpu.SemaphoreType.DMA((2, 3)),
         ],
         compiler_params=pltpu.CompilerParams(
             collective_id=0, has_side_effects=True, vmem_limit_bytes=40 * 1024 * 1024
         ),
     )(
-        *(pltpu.with_memory_space_constraint(x, pltpu.HBM) for x in (volume, conv4_weight.reshape(27 * CIN, C4), jnp.swapaxes(conv5_weight, 3, 4))),
+        *(pltpu.with_memory_space_constraint(x, pltpu.HBM) for x in (volume, conv4_weight.reshape(27 * CIN, C4), jnp.swapaxes(conv5_weight, 3, 4).reshape(3, 9, FILTERS, C4))),
     )
     cells = packed.reshape(4, 2, PLANE, 4, FILTERS).transpose(0, 3, 1, 2, 4)
     return cells.reshape(1, PLANE, PLANE, FILTERS)

time: 27.5 us -> 25.8 us (0.938)
  Pallas kernels: 26.5 us -> 24.7 us
    pallas_call x1, Pallas kernels: 26.5 us -> 24.7 us  [body(): pl.pallas_call(functools.partial(kernel, sizes), out_shape=jax.ShapeDtype...]
where the time goes in v4:
time: 25.8 us; the launch traced here: 25.6 us
  Pallas kernels  24.7 us (96%)
  local copies, waits for them, and re-layouts  0.9 us (3%)
    pallas_call x1, Pallas kernels, body(): pl.pallas_call(functools.partial(kernel, sizes), out_shape=jax.ShapeDtype...  24.7 us
    transpose x1, local copies, waits for them, and re-layouts, body(): cells = packed.reshape(4, 2, PLANE, 4, FILTERS).transpose(0, 3, 1, 2, 4)  0.75 us

profile of v4, /device:TPU:1, one launch (start us, length us, event | category | flops | bytes accessed | tf_op | source)
XLA Modules:
  0.0 25.6 jit_solution(2078845291654191337)
XLA Ops:
  0.0 24.7 %shard_map.37 = bf16[2,2,64,128]{3,2,1,0:T(8,128)(2,1)S(1)} custom-call(bf16[2,16,16,128]{3,2,1,0:T(8,128)(2,1)} %v.1, bf16[3456,256]{1,0:T(8,128)(2,1)} %bitcast.8, bf16[3,9,32,256]{3,2,1,0:T(8,128)(2,1)} %bitcast.10), custom_call_target="tpu_custom_call" | custom-call | tf_op jit(solution)/shard_map/pallas_call | solution.py:406
  24.7 0.2 reshape.14
  24.9 0.8 %copy.4 = bf16[4,4,2,32,32]{4,3,2,1,0:T(8,128)(2,1)} copy(bf16[4,4,2,32,32]{4,1,3,2,0:T(4,128)(2,1)S(1)} %bitcast.9) | data formatting | bytes 131072 | tf_op jit(solution)/shard_map/transpose | solution.py:452

commit v5 on v4

--- a/solution.py
+++ b/solution.py
@@ -17,7 +17,7 @@
 def kernel(
     sizes, v, w4, w5, out,
     pad, wide, taps, w4b, w5b, zs, yz, zh, ch, hidden, early, late, pool, block, blocks, rim, rims, slab, broad, sent, got, packed,
-    load_sem, halo_send, halo_recv, block_send, block_recv, rim_send, rim_recv, part_send, part_recv, shard_send, shard_recv,
+    known, load_sem, halo_send, halo_recv, block_send, block_recv, rim_send, rim_recv, part_send, part_recv, shard_send, shard_recv,
 ):
     ngx, ngy, ngz = sizes
     g, a, b = lax.axis_index("gx"), lax.axis_index("gy"), lax.axis_index("gz")
@@ -48,21 +48,16 @@
         load.start()
 
     barrier = pltpu.get_barrier_semaphore()
-    near_a = {da: lax.rem(a + da + ngy, ngy) for da in (-1, 0, 1)}
-    near_b = {db: lax.rem(b + db + ngz, ngz) for db in (-1, 0, 1)}
-
-    def greet(dg):
-        for da, db in sorted(((i, j) for i in (-1, 0, 1) for j in (-1, 0, 1)), key=lambda at: -abs(at[0]) - abs(at[1])):
-            if (dg, da, db) != (0, 0, 0):
-                pl.semaphore_signal(
-                    barrier, inc=1, device_id={"gx": g + dg, "gy": near_a[da], "gz": near_b[db]}, device_id_type=MESH
-                )
-
-    pl.when(g < ngx - 1)(lambda: greet(1))
-    pl.when(g > 0)(lambda: greet(-1))
-    greet(0)
-    sides = (g > 0).astype(jnp.int32) + (g < ngx - 1).astype(jnp.int32)
-    greeted = 9 * sides + 8
+    for shift in sorted(SHIFTS, key=lambda shift: -sum(map(abs, shift))):
+        @pl.when(there(*shift))
+        def _():
+            pl.semaphore_signal(barrier, inc=1, device_id=device(*shift), device_id_type=MESH)
+    pl.semaphore_signal(barrier, inc=1, device_id={"gy": other}, device_id_type=MESH)
+
+    def near(position, n):
+        return 1 + (position > 0).astype(jnp.int32) + (position < n - 1).astype(jnp.int32)
+
+    greeted = near(g, ngx) * near(a, ngy) * near(b, ngz)
 
     def finish(stage):
         if stage < 2:
@@ -220,6 +215,10 @@
         return jnp.concatenate([taps[x, dy * 16 : dy * 16 + 256, :] for dy in range(3)], axis=-1)
 
     halo_wait([shift for shift in SHIFTS if shift[0] == 0])
+    for db in (-1, 1):
+        @pl.when(there(0, 0, db))
+        def _():
+            pl.semaphore_signal(known, inc=1, device_id=device(0, 0, db), device_id_type=MESH)
     for x in (1, 2):
         widen(x)
     w4_load.wait()
@@ -262,6 +261,8 @@
         @pl.when(a == at)
         def _():
             rim[...] = block[first : first + 8, :]
+
+    pl.semaphore_wait(known, near(b, ngz) - 1)
 
     @pl.when(jnp.logical_or(a == 1, a == 2))
     def _():
@@ -431,6 +432,7 @@
             pltpu.VMEM((2, 3, 2, 64, 128), BF16),
             pltpu.VMEM((2, 3, 2, 64, 128), BF16),
             pltpu.VMEM((2, 2, 64, 128), F32),
+            pltpu.SemaphoreType.REGULAR,
             pltpu.SemaphoreType.DMA((5,)),
             pltpu.SemaphoreType.DMA((26,)),
             pltpu.SemaphoreType.DMA((26,)),

time: 25.8 us -> 25.3 us (0.981)
  Pallas kernels: 24.7 us -> 24.2 us
    pallas_call x1, Pallas kernels: 24.7 us -> 24.2 us  [body(): pl.pallas_call(functools.partial(kernel, sizes), out_shape=jax.ShapeDtype...]
where the time goes in v5:
time: 25.3 us; the launch traced here: 25.1 us
  Pallas kernels  24.2 us (96%)
  local copies, waits for them, and re-layouts  0.9 us (4%)
    pallas_call x1, Pallas kernels, body(): pl.pallas_call(functools.partial(kernel, sizes), out_shape=jax.ShapeDtype...  24.2 us
    transpose x1, local copies, waits for them, and re-layouts, body(): cells = packed.reshape(4, 2, PLANE, 4, FILTERS).transpose(0, 3, 1, 2, 4)  0.75 us

profile of v5, /device:TPU:1, one launch (start us, length us, event | category | flops | bytes accessed | tf_op | source)
XLA Modules:
  0.0 25.1 jit_solution(8017578689684434980)
XLA Ops:
  0.0 24.2 %shard_map.37 = bf16[2,2,64,128]{3,2,1,0:T(8,128)(2,1)S(1)} custom-call(bf16[2,16,16,128]{3,2,1,0:T(8,128)(2,1)} %v.1, bf16[3456,256]{1,0:T(8,128)(2,1)} %bitcast.8, bf16[3,9,32,256]{3,2,1,0:T(8,128)(2,1)} %bitcast.10), custom_call_target="tpu_custom_call" | custom-call | tf_op jit(solution)/shard_map/pallas_call | solution.py:407
  24.2 0.2 reshape.14
  24.4 0.8 %copy.4 = bf16[4,4,2,32,32]{4,3,2,1,0:T(8,128)(2,1)} copy(bf16[4,4,2,32,32]{4,1,3,2,0:T(4,128)(2,1)S(1)} %bitcast.9) | data formatting | bytes 131072 | tf_op jit(solution)/shard_map/transpose | solution.py:454

commit v6 on v5

--- a/solution.py
+++ b/solution.py
@@ -76,11 +76,10 @@
         if stage == 4:
             spread_sent()
         if stage >= 5:
-            for p, k in parts:
+            for k in range(3):
                 @part_when(k, True)
                 def _():
-                    for q in range(2):
-                        part_copy(p, k, q).wait_send()
+                    some_of(sent.at[1, 1] if k == 1 else sent.at[:, k], part_send.at[k]).wait_send()
 
     yz[...] = jnp.zeros(yz.shape, F32)
     own_load.wait()
@@ -245,15 +244,19 @@
     offsets = [(di, db) for di in range(2) for db in range(ngz) if (di, db) != (0, 0)]
 
     def spread(di, db):
-        number = di * ngz + db
-        return pltpu.make_async_remote_copy(
-            src_ref=block, dst_ref=blocks.at[mine], send_sem=block_send.at[number], recv_sem=block_recv.at[number],
+        return pltpu.make_async_remote_copy(
+            src_ref=block, dst_ref=blocks.at[mine], send_sem=block_send, recv_sem=block_recv.at[di],
             device_id={"gy": beside if di else a, "gz": lax.rem(b + db, ngz)}, device_id_type=MESH,
         )
 
+    def some_of(ref, sem):
+        return pltpu.make_async_remote_copy(
+            src_ref=ref, dst_ref=ref, send_sem=sem, recv_sem=sem, device_id={"gz": lax.rem(b + 1, ngz)}, device_id_type=MESH
+        )
+
     def rim_copy(t, db):
         return pltpu.make_async_remote_copy(
-            src_ref=rim, dst_ref=rims.at[b], send_sem=rim_send.at[t, db], recv_sem=rim_recv.at[db],
+            src_ref=rim, dst_ref=rims.at[b], send_sem=rim_send, recv_sem=rim_recv,
             device_id={"gy": 2 * (1 - half) + t, "gz": lax.rem(b + db, ngz)}, device_id_type=MESH,
         )
 
@@ -283,14 +286,11 @@
         for piece in range(3):
             shard_copy(piece).wait_send()
             shard_relay(piece).wait_send()
-        for di, db in offsets:
-            spread(di, db).wait_send()
+        some_of(blocks.at[0:7], block_send).wait_send()
 
         @pl.when(jnp.logical_or(a == 1, a == 2))
         def _():
-            for t in range(2):
-                for db in range(ngz):
-                    rim_copy(t, db).wait_send()
+            some_of(block, rim_send).wait_send()
 
     def lay(first, rows):
         for dz in range(3):
@@ -301,9 +301,7 @@
     taps_w5 = (((1,), (1,)), ((), ()))
 
     def settle(di, row):
-        for db in range(ngz):
-            if (di, db) != (0, 0):
-                spread(di, db).wait_recv()
+        some_of(blocks.at[pl.ds(4 * row, 4)] if di else blocks.at[0:3], block_recv.at[di]).wait_recv()
         for z in range(ngz):
             broad[pl.ds(1 + 8 * row, 8), 8 + 8 * z : 16 + 8 * z, :] = blocks[row * ngz + z].astype(F32).reshape(8, 8, C4)
         lay(1 + 8 * row, 8)
@@ -327,8 +325,7 @@
             rows_of(8 * at + 4 * part, 4), all_taps(range(9)), taps_w5, preferred_element_type=F32
         )
     settle(1, 1 - at)
-    for db in range(ngz):
-        rim_copy(0, db).wait_recv()
+    some_of(rims, rim_recv).wait_recv()
     for z in range(ngz):
         broad[17 * (1 - half), 8 + 8 * z : 16 + 8 * z, :] = rims[z].astype(F32)
     lay(17 * (1 - half), 1)
@@ -344,7 +341,7 @@
 
     def part_copy(p, k, q):
         return pltpu.make_async_remote_copy(
-            src_ref=sent.at[p, k, q], dst_ref=got.at[p, k, q], send_sem=part_send.at[p, k, q], recv_sem=part_recv.at[p, k, q],
+            src_ref=sent.at[p, k, q], dst_ref=got.at[p, k, q], send_sem=part_send.at[k], recv_sem=part_recv.at[k],
             device_id={"gx": g + 1 - k, "gy": other if p else a}, device_id_type=MESH,
         )
 
@@ -383,16 +380,13 @@
     send_parts(late[...], 1)
 
     spread_sent()
-    for slot in range(2):
-        part_copy(1, 1, slot).wait_recv()
-        packed[1, slot] = got[1, 1, slot].astype(F32)
+    some_of(got.at[1, 1], part_recv.at[1]).wait_recv()
+    packed[1] = got[1, 1].astype(F32)
     for k in (0, 2):
         @part_when(k, False)
         def _():
-            for p in range(2):
-                for slot in range(2):
-                    part_copy(p, k, slot).wait_recv()
-                    packed[p, slot] += got[p, k, slot].astype(F32)
+            some_of(got.at[:, k], part_recv.at[k]).wait_recv()
+            packed[...] += got[:, k].astype(F32)
 
     for p, place in ((0, half), (1, 1 - half)):
         for slot in range(2):
@@ -436,12 +430,12 @@
             pltpu.SemaphoreType.DMA((5,)),
             pltpu.SemaphoreType.DMA((26,)),
             pltpu.SemaphoreType.DMA((26,)),
-            pltpu.SemaphoreType.DMA((2 * ngz,)),
-            pltpu.SemaphoreType.DMA((2 * ngz,)),
-            pltpu.SemaphoreType.DMA((2, ngz)),
-            pltpu.SemaphoreType.DMA((ngz,)),
-            pltpu.SemaphoreType.DMA((2, 3, 2)),
-            pltpu.SemaphoreType.DMA((2, 3, 2)),
+            pltpu.SemaphoreType.DMA,
+            pltpu.SemaphoreType.DMA((2,)),
+            pltpu.SemaphoreType.DMA,
+            pltpu.SemaphoreType.DMA,
+            pltpu.SemaphoreType.DMA((3,)),
+            pltpu.SemaphoreType.DMA((3,)),
             pltpu.SemaphoreType.DMA((2, 3)),
             pltpu.SemaphoreType.DMA((2, 3)),
         ],

time: 25.3 us -> 24.9 us (0.984)
  Pallas kernels: 24.2 us -> 23.8 us
    pallas_call x1, Pallas kernels: 24.2 us -> 23.8 us  [body(): pl.pallas_call(functools.partial(kernel, sizes), out_shape=jax.ShapeDtype...]
where the time goes in v6:
time: 24.9 us; the launch traced here: 24.8 us
  Pallas kernels  23.8 us (96%)
  local copies, waits for them, and re-layouts  0.9 us (4%)
    pallas_call x1, Pallas kernels, body(): pl.pallas_call(functools.partial(kernel, sizes), out_shape=jax.ShapeDtype...  23.8 us
    transpose x1, local copies, waits for them, and re-layouts, body(): cells = packed.reshape(4, 2, PLANE, 4, FILTERS).transpose(0, 3, 1, 2, 4)  0.75 us

profile of v6, /device:TPU:1, one launch (start us, length us, event | category | flops | bytes accessed | tf_op | source)
XLA Modules:
  0.0 24.8 jit_solution(4722677310998907557)
XLA Ops:
  0.0 23.8 %shard_map.37 = bf16[2,2,64,128]{3,2,1,0:T(8,128)(2,1)S(1)} custom-call(bf16[2,16,16,128]{3,2,1,0:T(8,128)(2,1)} %v.1, bf16[3456,256]{1,0:T(8,128)(2,1)} %bitcast.8, bf16[3,9,32,256]{3,2,1,0:T(8,128)(2,1)} %bitcast.10), custom_call_target="tpu_custom_call" | custom-call | tf_op jit(solution)/shard_map/pallas_call | solution.py:401
  23.8 0.2 reshape.14
  24.0 0.8 %copy.4 = bf16[4,4,2,32,32]{4,3,2,1,0:T(8,128)(2,1)} copy(bf16[4,4,2,32,32]{4,1,3,2,0:T(4,128)(2,1)S(1)} %bitcast.9) | data formatting | bytes 131072 | tf_op jit(solution)/shard_map/transpose | solution.py:448

commit v7 on v6

--- a/solution.py
+++ b/solution.py
@@ -177,14 +177,14 @@
     def shard_copy(piece):
         return pltpu.make_async_remote_copy(
             src_ref=shard_rows(0, piece), dst_ref=shard_rows(96, piece),
-            send_sem=shard_send.at[0, piece], recv_sem=shard_recv.at[0, piece],
+            send_sem=shard_send.at[0], recv_sem=shard_recv.at[0, piece],
             device_id={"gy": other}, device_id_type=MESH,
         )
 
     def shard_relay(piece):
         return pltpu.make_async_remote_copy(
             src_ref=shard_rows(96, piece), dst_ref=shard_rows(96, piece),
-            send_sem=shard_send.at[1, piece], recv_sem=shard_recv.at[1, piece],
+            send_sem=shard_send.at[1], recv_sem=shard_recv.at[1, 0],
             device_id={"gx": g + 1 - 2 * core}, device_id_type=MESH,
         )
 
@@ -283,9 +283,8 @@
         shard_relay(piece).start()
 
     def spread_sent():
-        for piece in range(3):
-            shard_copy(piece).wait_send()
-            shard_relay(piece).wait_send()
+        for kind in range(2):
+            some_of(w5b.at[:, 0:48], shard_send.at[kind]).wait_send()
         some_of(blocks.at[0:7], block_send).wait_send()
 
         @pl.when(jnp.logical_or(a == 1, a == 2))
@@ -318,8 +317,7 @@
     for dz in range(3):
         for row in (8 * at, 8 * at + 9):
             slab[dz, row] = jnp.zeros((PLANE, C4), BF16)
-    for piece in range(3):
-        shard_relay(piece).wait_recv()
+    some_of(w5b.at[:, 0:48], shard_recv.at[1, 0]).wait_recv()
     for part in range(2):
         early[128 * part : 128 * part + 128, :192] = lax.dot_general(
             rows_of(8 * at + 4 * part, 4), all_taps(range(9)), taps_w5, preferred_element_type=F32
@@ -436,7 +434,7 @@
             pltpu.SemaphoreType.DMA,
             pltpu.SemaphoreType.DMA((3,)),
             pltpu.SemaphoreType.DMA((3,)),
-            pltpu.SemaphoreType.DMA((2, 3)),
+            pltpu.SemaphoreType.DMA((2,)),
             pltpu.SemaphoreType.DMA((2, 3)),
         ],
         compiler_params=pltpu.CompilerParams(

time: 24.9 us -> 24.8 us (level)
  no operation moved by 1% of the time
where the time goes in v7:
time: 24.8 us; the launch traced here: 24.7 us
  Pallas kernels  23.8 us (96%)
  local copies, waits for them, and re-layouts  0.9 us (4%)
    pallas_call x1, Pallas kernels, body(): pl.pallas_call(functools.partial(kernel, sizes), out_shape=jax.ShapeDtype...  23.8 us
    transpose x1, local copies, waits for them, and re-layouts, body(): cells = packed.reshape(4, 2, PLANE, 4, FILTERS).transpose(0, 3, 1, 2, 4)  0.75 us

profile of v7, /device:TPU:1, one launch (start us, length us, event | category | flops | bytes accessed | tf_op | source)
XLA Modules:
  0.0 24.7 jit_solution(11085832552512912346)
XLA Ops:
  0.0 23.8 %shard_map.37 = bf16[2,2,64,128]{3,2,1,0:T(8,128)(2,1)S(1)} custom-call(bf16[2,16,16,128]{3,2,1,0:T(8,128)(2,1)} %v.1, bf16[3456,256]{1,0:T(8,128)(2,1)} %bitcast.8, bf16[3,9,32,256]{3,2,1,0:T(8,128)(2,1)} %bitcast.10), custom_call_target="tpu_custom_call" | custom-call | tf_op jit(solution)/shard_map/pallas_call | solution.py:399
  23.8 0.2 reshape.14
  23.9 0.8 %copy.4 = bf16[4,4,2,32,32]{4,3,2,1,0:T(8,128)(2,1)} copy(bf16[4,4,2,32,32]{4,1,3,2,0:T(4,128)(2,1)S(1)} %bitcast.9) | data formatting | bytes 131072 | tf_op jit(solution)/shard_map/transpose | solution.py:446

commit v8 on v7

--- a/solution.py
+++ b/solution.py
@@ -17,7 +17,7 @@
 def kernel(
     sizes, v, w4, w5, out,
     pad, wide, taps, w4b, w5b, zs, yz, zh, ch, hidden, early, late, pool, block, blocks, rim, rims, slab, broad, sent, got, packed,
-    known, load_sem, halo_send, halo_recv, block_send, block_recv, rim_send, rim_recv, part_send, part_recv, shard_send, shard_recv,
+    known, load_sem, halo_send, halo_recv, block_send, block_recv, rim_send, rim_recv, part_recv, shard_send, shard_recv,
 ):
     ngx, ngy, ngz = sizes
     g, a, b = lax.axis_index("gx"), lax.axis_index("gy"), lax.axis_index("gz")
@@ -79,7 +79,7 @@
             for k in range(3):
                 @part_when(k, True)
                 def _():
-                    some_of(sent.at[1, 1] if k == 1 else sent.at[:, k], part_send.at[k]).wait_send()
+                    some_of(sent.at[1, 1] if k == 1 else sent.at[:, k], halo_send.at[k]).wait_send()
 
     yz[...] = jnp.zeros(yz.shape, F32)
     own_load.wait()
@@ -339,7 +339,7 @@
 
     def part_copy(p, k, q):
         return pltpu.make_async_remote_copy(
-            src_ref=sent.at[p, k, q], dst_ref=got.at[p, k, q], send_sem=part_send.at[k], recv_sem=part_recv.at[k],
+            src_ref=sent.at[p, k, q], dst_ref=got.at[p, k, q], send_sem=halo_send.at[k], recv_sem=part_recv.at[k],
             device_id={"gx": g + 1 - k, "gy": other if p else a}, device_id_type=MESH,
         )
 
@@ -433,7 +433,6 @@
             pltpu.SemaphoreType.DMA,
             pltpu.SemaphoreType.DMA,
             pltpu.SemaphoreType.DMA((3,)),
-            pltpu.SemaphoreType.DMA((3,)),
             pltpu.SemaphoreType.DMA((2,)),
             pltpu.SemaphoreType.DMA((2, 3)),
         ],

time: 24.8 us -> 24.8 us (level)
  no operation moved by 1% of the time
where the time goes in v8:
time: 24.8 us; the launch traced here: 24.7 us
  Pallas kernels  23.8 us (96%)
  local copies, waits for them, and re-layouts  0.9 us (4%)
    pallas_call x1, Pallas kernels, body(): pl.pallas_call(functools.partial(kernel, sizes), out_shape=jax.ShapeDtype...  23.8 us
    transpose x1, local copies, waits for them, and re-layouts, body(): cells = packed.reshape(4, 2, PLANE, 4, FILTERS).transpose(0, 3, 1, 2, 4)  0.75 us

profile of v8, /device:TPU:1, one launch (start us, length us, event | category | flops | bytes accessed | tf_op | source)
XLA Modules:
  0.0 24.7 jit_solution(6390774063625479056)
XLA Ops:
  0.0 23.8 %shard_map.37 = bf16[2,2,64,128]{3,2,1,0:T(8,128)(2,1)S(1)} custom-call(bf16[2,16,16,128]{3,2,1,0:T(8,128)(2,1)} %v.1, bf16[3456,256]{1,0:T(8,128)(2,1)} %bitcast.8, bf16[3,9,32,256]{3,2,1,0:T(8,128)(2,1)} %bitcast.10), custom_call_target="tpu_custom_call" | custom-call | tf_op jit(solution)/shard_map/pallas_call | solution.py:399
  23.8 0.2 reshape.14
  23.9 0.8 %copy.4 = bf16[4,4,2,32,32]{4,3,2,1,0:T(8,128)(2,1)} copy(bf16[4,4,2,32,32]{4,1,3,2,0:T(4,128)(2,1)S(1)} %bitcast.9) | data formatting | bytes 131072 | tf_op jit(solution)/shard_map/transpose | solution.py:445
